TPU v7x, 256 devices: a whole 4x4x8 slice. The times are simulated.
256 devices in a mesh: row: 16 (over x_lo, y, core), col: 16 (over x_hi, z).
Axes of the slice: x: 4 (x_hi: 2, x_lo: 2; x = x_hi * 2 + x_lo), y: 4, z: 8, core: 2. Of those that a mesh axis runs over, the one named last changes fastest.
Arguments:
- node_features: bfloat16 [65536, 256], P(('row', 'col')), may hold values from -6 to 6
- tile_values: bfloat16 [16, 16, 128, 128, 128], P('row', 'col'), may hold values from -0.09375 to 0.09375
- tile_coords: int32 [16, 16, 128, 2], P('row', 'col'), may hold values from 0 to 31, as said below
- tile_counts: int32 [16, 16], P('row', 'col'), may hold values from 32 to 128, as said below
- first_weight: bfloat16 [256, 256], replicated, may hold values from -0.375 to 0.375
- second_weight: bfloat16 [256, 128], replicated, may hold values from -0.375 to 0.375
- out_grad: bfloat16 [65536, 128], P(('row', 'col')), may hold values from -6 to 6
Outputs:
- output: bfloat16 [65536, 128], P(('row', 'col'))
- first_grad: float32 [256, 256], replicated
- second_grad: float32 [256, 128], replicated
Inputs may be any that keep to these rules, and one draw needn't show every extreme that they name: `tile_counts`: each grid cell uses at least 32 slots; at least one grid cell uses all 128 in every draw. `tile_coords`: the first entry is a tile row below 32, the second a tile column below 32; within one grid cell no two slots share a position.
All inputs are finite; a program needn't handle non-finite values.
Results may differ from a plain program's by a relative error of at most 0.005.
Values may be sent and summed in bfloat16 or wider, within the bound.
A program may use at most 64 MiB of HBM per device.

v0:
```python
import math

import jax
import jax.numpy as jnp
from jax import lax
from jax.sharding import PartitionSpec as P

HIGHEST = lax.Precision.HIGHEST


def tile_sum(tile_block, dest_index, source_index, live_slots, source, dest_tiles, flipped):
    slot_count = tile_block.shape[0]
    group_size = math.gcd(slot_count, 32)
    round_count = slot_count // group_size
    edge_size = tile_block.shape[1]
    width_size = source.shape[-1]
    grouped_tiles = tile_block.reshape(round_count, group_size, edge_size, edge_size)
    grouped_dest = dest_index.reshape(round_count, group_size)
    grouped_source = source_index.reshape(round_count, group_size)
    grouped_live = live_slots.reshape(round_count, group_size)
    target_ids = jnp.arange(dest_tiles, dtype=jnp.int32)
    einsum_form = "tba,tbw->taw" if flipped else "tab,tbw->taw"

    def add_group(running, pieces):
        group_tiles, group_dest, group_source, group_live = pieces
        picked = jnp.take(source, group_source, axis=0)
        products = jnp.einsum(einsum_form, group_tiles, picked, preferred_element_type=jnp.float32)
        select = ((group_dest[:, None] == target_ids[None, :]) & group_live[:, None]).astype(
            jnp.float32
        )
        running = running + jnp.einsum("tr,taw->raw", select, products, precision=HIGHEST)
        return (running, None)

    start_sum = jnp.zeros((dest_tiles, edge_size, width_size), jnp.float32)
    running, unused = lax.scan(
        add_group, start_sum, (grouped_tiles, grouped_dest, grouped_source, grouped_live)
    )
    return running.reshape(dest_tiles * edge_size, width_size)


def on_device(
    node_features, tile_values, tile_coords, tile_counts, first_weight, second_weight, out_grad
):
    node_rows = node_features.shape[0]
    edge_size = tile_values.shape[-1]
    slot_count = tile_values.shape[2]
    grid_rows = lax.axis_size("row")
    grid_cols = lax.axis_size("col")
    row_tiles = grid_rows * node_rows // edge_size
    col_tiles = grid_cols * node_rows // edge_size
    tile_block = tile_values.reshape(slot_count, edge_size, edge_size)
    flat_coords = tile_coords.reshape(slot_count, 2)
    tile_row = flat_coords[:, 0]
    tile_col = flat_coords[:, 1]
    live_slots = jnp.arange(slot_count, dtype=jnp.int32) < tile_counts.reshape(())
    gathered_x = lax.all_gather(node_features, "col", axis=0, tiled=True)
    feature_part = tile_sum(
        tile_block,
        tile_row,
        tile_col,
        live_slots,
        gathered_x.reshape(col_tiles, edge_size, -1),
        row_tiles,
        False,
    )
    first_mean = lax.psum_scatter(feature_part, "row", scatter_dimension=0, tiled=True)
    first_pre = jnp.dot(first_mean, first_weight.astype(jnp.float32), precision=HIGHEST)
    hidden_act = jax.nn.silu(first_pre).astype(jnp.bfloat16)
    second_wide = second_weight.astype(jnp.float32)
    gathered_h = lax.all_gather(hidden_act, "col", axis=0, tiled=True)
    hidden_part = tile_sum(
        tile_block,
        tile_row,
        tile_col,
        live_slots,
        gathered_h.reshape(col_tiles, edge_size, -1),
        row_tiles,
        False,
    )
    second_mean = lax.psum_scatter(hidden_part, "row", scatter_dimension=0, tiled=True)
    logit_rows = jnp.dot(second_mean, second_wide, precision=HIGHEST)
    output = logit_rows.astype(jnp.bfloat16)
    gathered_g = lax.all_gather(out_grad, "row", axis=0, tiled=True)
    grad_part = tile_sum(
        tile_block,
        tile_col,
        tile_row,
        live_slots,
        gathered_g.reshape(row_tiles, edge_size, -1),
        col_tiles,
        True,
    )
    back_sum = lax.psum_scatter(grad_part, "col", scatter_dimension=0, tiled=True)
    scale = 1.0 / math.sqrt(node_rows * grid_rows * grid_cols)
    second_local = jnp.dot(hidden_act.astype(jnp.float32).T, back_sum, precision=HIGHEST) * scale
    hidden_grad = jnp.dot(back_sum, second_wide.T, precision=HIGHEST)
    sigma = jax.nn.sigmoid(first_pre)
    pre_grad = hidden_grad * (sigma * (1.0 + first_pre * (1.0 - sigma)))
    second_grad = lax.psum(second_local, ("row", "col"))
    first_local = jnp.dot(first_mean.T, pre_grad, precision=HIGHEST) * scale
    first_grad = lax.psum(first_local, ("row", "col"))
    return (output, first_grad, second_grad)


def solution(mesh):
    return jax.shard_map(
        on_device,
        mesh=mesh,
        in_specs=(
            P(("row", "col"), None),
            P("row", "col", None, None, None),
            P("row", "col", None, None),
            P("row", "col"),
            P(),
            P(),
            P(("row", "col"), None),
        ),
        out_specs=(P(("row", "col"), None), P(), P()),
        check_vma=False,
    )
```

profile of v0, /device:TPU:1, one launch (start us, length us, event | category | flops | bytes accessed | tf_op | source)
XLA Modules:
  0.0 898.8 jit_solution(9143985936863349914)
XLA Ops:
  9.6 86.8 %all-gather.4.cloned.1.call-done = bf16[4096,256]{1,0:T(8,128)(2,1)} async-done(((bf16[256,256]{1,0:T(8,128)(2,1)}), bf16[4096,256]{1,0:T(8,128)(2,1)}) %all-gather.4.cloned.1.call-update) | async-done | bytes 2097168 | tf_op jit(solution)/shard_map/all_gather | solution.py:56
  96.3 64.7 %while.33 = (s32[]{:T(128)}, f32[32,128,256]{2,0,1:T(8,128)}, s32[4,32]{1,0:T(4,128)S(1)}, pred[4,32]{1,0:T(4,128)(4,1)S(1)}, bf16[4,32,128,128]{3,2,1,0:T(8,128...) while((s32[]{:T(128)}, f32[32,128,256]{2,0,1:T(8,128)}, ...), condition=%wide.region_1.3_spmd.clone, body=%wide.region_0.2_spmd.clone.sunk | while | flops 674237632 | bytes 24123028 | solution.py:35
  98.6 4.0 fusion.96
  102.6 8.9 select_add_fusion.6
  113.9 4.0 fusion.96
  117.9 10.2 %select_add_fusion.6 = f32[32,128,256]{2,0,1:T(8,128)} fusion(f32[32,128,256]{2,0,1:T(8,128)} %get-tuple-element.410, f32[32,128,256]{2,1,0:T(8,128)} %fusion.96, pred[]{:T(512)S(6)} %compare.9, s32[32]{0:T(128)S(1)} %fusion.97, pred[32]{0:T(512)(128)(4,1)S(1)} %dynamic-slice_bitcast_fusion.6), kind=kOutput, calls=%fused_computation.33.clone.1 | convolution fusion | flops 404752384 | bytes 12583073 | tf_op jit(solution)/shard_map/while/body/eval_jaxpr/tr,taw->raw/dot_general | solution.py:31
  130.4 4.0 fusion.96
  134.4 10.2 %select_add_fusion.6 = f32[32,128,256]{2,0,1:T(8,128)} fusion(f32[32,128,256]{2,0,1:T(8,128)} %get-tuple-element.410, f32[32,128,256]{2,1,0:T(8,128)} %fusion.96, pred[]{:T(512)S(6)} %compare.9, s32[32]{0:T(128)S(1)} %fusion.97, pred[32]{0:T(512)(128)(4,1)S(1)} %dynamic-slice_bitcast_fusion.6), kind=kOutput, calls=%fused_computation.33.clone.1 | convolution fusion | flops 404752384 | bytes 12583073 | tf_op jit(solution)/shard_map/while/body/eval_jaxpr/tr,taw->raw/dot_general | solution.py:31
  146.9 4.0 fusion.96
  150.9 10.2 %select_add_fusion.6 = f32[32,128,256]{2,0,1:T(8,128)} fusion(f32[32,128,256]{2,0,1:T(8,128)} %get-tuple-element.410, f32[32,128,256]{2,1,0:T(8,128)} %fusion.96, pred[]{:T(512)S(6)} %compare.9, s32[32]{0:T(128)S(1)} %fusion.97, pred[32]{0:T(512)(128)(4,1)S(1)} %dynamic-slice_bitcast_fusion.6), kind=kOutput, calls=%fused_computation.33.clone.1 | convolution fusion | flops 404752384 | bytes 12583073 | tf_op jit(solution)/shard_map/while/body/eval_jaxpr/tr,taw->raw/dot_general | solution.py:31
  161.0 6.6 copy.10
  168.5 65.5 %reduce-scatter.4.cloned.1.call-done = f32[256,256]{1,0:T(8,128)} async-done(((f32[4096,256]{1,0:T(8,128)}), f32[256,256]{1,0:T(8,128)}) %reduce-scatter.4.cloned.1.call-update) | async-done | bytes 262160 | tf_op jit(solution)/shard_map/reduce_scatter | solution.py:66
  236.2 37.0 %all-gather.8.cloned.1.call-done = bf16[4096,128]{1,0:T(8,128)(2,1)} async-done(((bf16[256,128]{1,0:T(8,128)(2,1)}), bf16[4096,128]{1,0:T(8,128)(2,1)}) %all-gather.8.cloned.1.call-update) | async-done | bytes 1048592 | tf_op jit(solution)/shard_map/all_gather | solution.py:83
  273.2 35.7 %while.35 = (s32[]{:T(128)}, f32[32,128,128]{2,0,1:T(8,128)}, s32[4,32]{1,0:T(4,128)S(1)}, pred[4,32]{1,0:T(4,128)(4,1)S(1)}, bf16[4,32,128,128]{3,2,1,0:T(8,128...) while((s32[]{:T(128)}, f32[32,128,128]{2,0,1:T(8,128)}, ...), condition=%wide.region_7.9_spmd.clone, body=%wide.region_6.8_spmd.clone.sunk | while | flops 337120544 | bytes 12588823 | solution.py:35
  284.7 5.4 select_add_fusion.8
  294.0 5.5 select_add_fusion.8
  303.4 5.5 select_add_fusion.8
  308.8 4.2 copy.12
  313.0 44.8 %all-gather.6.cloned.1.call-done = bf16[4096,256]{1,0:T(8,128)(2,1)} async-done(((bf16[256,256]{1,0:T(8,128)(2,1)}), bf16[4096,256]{1,0:T(8,128)(2,1)}) %all-gather.6.cloned.1.call-update) | async-done | bytes 2097168 | tf_op jit(solution)/shard_map/all_gather | solution.py:70
  357.8 65.0 %while.34 = (s32[]{:T(128)}, f32[32,128,256]{2,0,1:T(8,128)}, s32[4,32]{1,0:T(4,128)S(1)}, pred[4,32]{1,0:T(4,128)(4,1)S(1)}, bf16[4,32,128,128]{3,2,1,0:T(8,128...) while((s32[]{:T(128)}, f32[32,128,256]{2,0,1:T(8,128)}, ...), condition=%wide.region_4.6_spmd.clone, body=%wide.region_3.5_spmd.clone.sunk | while | flops 674237632 | bytes 24123028 | solution.py:35
  360.1 4.0 fusion.102
  364.1 8.9 select_add_fusion.7
  375.4 4.0 fusion.102
  379.4 10.2 %select_add_fusion.7 = f32[32,128,256]{2,0,1:T(8,128)} fusion(f32[32,128,256]{2,0,1:T(8,128)} %get-tuple-element.437, f32[32,128,256]{2,1,0:T(8,128)} %fusion.102, pred[]{:T(512)S(6)} %compare.10, s32[32]{0:T(128)S(1)} %fusion.103, pred[32]{0:T(512)(128)(4,1)S(1)} %dynamic-slice_bitcast_fusion.7), kind=kOutput, calls=%fused_computation.57.clone.1 | convolution fusion | flops 404752384 | bytes 12583073 | tf_op jit(solution)/shard_map/while/body/eval_jaxpr/tr,taw->raw/dot_general | solution.py:31
  392.0 4.0 fusion.102
  396.0 10.3 %select_add_fusion.7 = f32[32,128,256]{2,0,1:T(8,128)} fusion(f32[32,128,256]{2,0,1:T(8,128)} %get-tuple-element.437, f32[32,128,256]{2,1,0:T(8,128)} %fusion.102, pred[]{:T(512)S(6)} %compare.10, s32[32]{0:T(128)S(1)} %fusion.103, pred[32]{0:T(512)(128)(4,1)S(1)} %dynamic-slice_bitcast_fusion.7), kind=kOutput, calls=%fused_computation.57.clone.1 | convolution fusion | flops 404752384 | bytes 12583073 | tf_op jit(solution)/shard_map/while/body/eval_jaxpr/tr,taw->raw/dot_general | solution.py:31
  408.6 4.0 fusion.102
  412.6 10.2 %select_add_fusion.7 = f32[32,128,256]{2,0,1:T(8,128)} fusion(f32[32,128,256]{2,0,1:T(8,128)} %get-tuple-element.437, f32[32,128,256]{2,1,0:T(8,128)} %fusion.102, pred[]{:T(512)S(6)} %compare.10, s32[32]{0:T(128)S(1)} %fusion.103, pred[32]{0:T(512)(128)(4,1)S(1)} %dynamic-slice_bitcast_fusion.7), kind=kOutput, calls=%fused_computation.57.clone.1 | convolution fusion | flops 404752384 | bytes 12583073 | tf_op jit(solution)/shard_map/while/body/eval_jaxpr/tr,taw->raw/dot_general | solution.py:31
  422.8 6.6 copy.11
  429.5 131.3 %reduce-scatter.8.cloned.1.call-done = f32[256,128]{1,0:T(8,128)} async-done(((f32[4096,128]{1,0:T(8,128)}), f32[256,128]{1,0:T(8,128)}) %reduce-scatter.8.cloned.1.call-update) | async-done | bytes 131088 | tf_op jit(solution)/shard_map/reduce_scatter | solution.py:93
  565.2 67.1 %reduce-scatter.6.cloned.1.call-done = f32[256,256]{1,0:T(8,128)} async-done(((f32[4096,256]{1,0:T(8,128)}), f32[256,256]{1,0:T(8,128)}) %reduce-scatter.6.cloned.1.call-update) | async-done | bytes 262160 | tf_op jit(solution)/shard_map/reduce_scatter | solution.py:80
  634.2 254.5 %all-reduce.3.cloned.1.call-done = (f32[256,256]{1,0:T(8,128)}, f32[256,128]{1,0:T(8,128)}) async-done(((f32[256,256]{1,0:T(8,128)}, f32[256,128]{1,0:T(8,128)}), (f32[256,256]{1,0:T(8,128)}, f32[256,128]{1,0:T(8,128)})) %all-reduce.3.cloned.1.call-update) | async-done | bytes 393232 | tf_op jit(solution)/shard_map/psum | solution.py:101
  (105 shorter events, 51.9 us)
Async XLA Ops:
  7.2 226.8 %copy-start = (bf16[256,256]{1,0:T(8,128)(2,1)S(1)}, bf16[256,256]{1,0:T(8,128)(2,1)}, u32[]{:S(2)}) copy-start(bf16[256,256]{1,0:T(8,128)(2,1)} %param.19) | copy-start | bytes 393220
  7.2 89.2 %all-gather.4.cloned.1.call-start = ((), (), s32[]{:S(2)}) async-start(), calls=%async_computation.3 | async-start | bytes 2228224 | tf_op jit(solution)/shard_map/all_gather | solution.py:56
  7.9 226.1 %reduce-scatter.4.cloned.1.call-start = ((), (), s32[]{:S(2)}) async-start(), calls=%async_computation.4 | async-start | bytes 4456448 | tf_op jit(solution)/shard_map/reduce_scatter | solution.py:66
  167.7 105.5 %all-gather.8.cloned.1.call-start = ((), (), s32[]{:S(2)}) async-start(), calls=%async_computation.7 | async-start | bytes 1114112 | tf_op jit(solution)/shard_map/all_gather | solution.py:83
  168.4 189.4 %all-gather.6.cloned.1.call-start = ((), (), s32[]{:S(2)}) async-start(), calls=%async_computation.5 | async-start | bytes 2228224 | tf_op jit(solution)/shard_map/all_gather | solution.py:70
  235.9 324.9 %reduce-scatter.8.cloned.1.call-start = ((), (), s32[]{:S(2)}) async-start(), calls=%async_computation.8 | async-start | bytes 2228224 | tf_op jit(solution)/shard_map/reduce_scatter | solution.py:93
  313.0 319.3 %reduce-scatter.6.cloned.1.call-start = ((), (), s32[]{:S(2)}) async-start(), calls=%async_computation.6 | async-start | bytes 4456448 | tf_op jit(solution)/shard_map/reduce_scatter | solution.py:80
  429.4 131.4 %copy-start.1 = (bf16[256,256]{1,0:T(8,128)(2,1)S(1)}, bf16[256,256]{1,0:T(8,128)(2,1)}, u32[]{:S(2)}) copy-start(bf16[256,256]{1,0:T(8,128)(2,1)} %get-tuple-element.261) | copy-start | bytes 393220
  429.4 133.3 %copy-start.3 = (bf16[256,128]{1,0:T(8,128)(2,1)S(1)}, bf16[256,128]{1,0:T(8,128)(2,1)}, u32[]{:S(2)}) copy-start(bf16[256,128]{1,0:T(8,128)(2,1)} %param.20) | copy-start | bytes 196612
  429.4 134.5 %copy-start.2 = (f32[256,256]{1,0:T(8,128)S(1)}, f32[256,256]{1,0:T(8,128)}, u32[]{:S(2)}) copy-start(f32[256,256]{1,0:T(8,128)} %reduce-scatter.4.cloned.1.call-done) | copy-start | bytes 786436
  429.4 459.3 %all-reduce.3.cloned.1.call-start = ((), (), s32[]{:S(2)}) async-start(), calls=%async_computation.9 | async-start | bytes 786432 | tf_op jit(solution)/shard_map/psum | solution.py:101
Sparse Core Ops, SparseCore 0:
  10.6 85.6 all-gather.3
  167.8 66.1 reduce-scatter.3
  235.9 37.2 all-gather.7
  276.2 81.5 all-gather.5
  361.5 199.2 reduce-scatter.7
  563.2 69.0 reduce-scatter.5
  638.4 250.2 all-reduce.2
where the time goes:
time: 900 us; the launch traced here: 899 us
  waiting for transfers between devices  688 us (76%)
  matrix products  147 us (16%)
  local copies, waits for them, and re-layouts  47.9 us (5%)
  between operations  14.8 us (2%)
    psum x1, waiting for transfers between devices, on_device(): first_grad = lax.psum(first_local, ('row', 'col'))  255 us
    reduce_scatter x1, waiting for transfers between devices, on_device(): lax.psum_scatter(grad_part, 'col', scatter_dimension=0, tiled=True)  131 us
    dot_general x12, matrix products, add_group(): jnp.einsum('tr,taw->raw', select, products, precision=HIGHEST)  99.3 us
    all_gather x1, waiting for transfers between devices, on_device(): gathered_x = lax.all_gather(node_features, 'col', axis=0, tiled=True)  86.8 us
    reduce_scatter x1, waiting for transfers between devices, on_device(): lax.psum_scatter(hidden_part, 'row', scatter_dimension=0, tiled=True)  67.1 us
    reduce_scatter x1, waiting for transfers between devices, on_device(): lax.psum_scatter(feature_part, 'row', scatter_dimension=0, tiled=True)  65.5 us
    all_gather x1, waiting for transfers between devices, on_device(): gathered_h = lax.all_gather(hidden_act, 'col', axis=0, tiled=True)  44.8 us
    dot_general x12, matrix products, add_group(): jnp.einsum(einsum_form, group_tiles, picked, preferred_element_type=jnp.f...  39.1 us
  transfers between devices with their start and end apart: 7, of which 7 were waited for; matrix products, arithmetic and copies ran while one was open for 13% of the time, Pallas kernels for 0%

commit v1 on v0

v1 whole, which is shorter than its diff:
```python
import functools
import math

import jax
import jax.numpy as jnp
from jax import lax
from jax.experimental import pallas as pl
from jax.experimental.pallas import tpu as pltpu
from jax.sharding import PartitionSpec as P

HIGHEST = lax.Precision.HIGHEST
MESH = pl.DeviceIdType.MESH
ANY = pl.BlockSpec(memory_space=pl.ANY)
WHOLE = pl.BlockSpec(memory_space=pltpu.VMEM)
DMA = pltpu.SemaphoreType.DMA
F32 = jnp.float32
BF16 = jnp.bfloat16

Y = 4
Z = 8
CHIPS = 8
ROW = 16
COL = 16
NEAR = ((1, 2), (1, 1), (1, 3), (0, 2), (0, 1), (0, 3), (1, 0))
OWN_UP, OWN_DOWN, FAR_UP, FAR_DOWN = 0, 1, 2, 3
STEPS = (4, 3, 3, 4)
TILES_AT_ONCE = 16
GROUP = 4


def where_am_i():
    row = lax.axis_index("row")
    col = lax.axis_index("col")
    core = lax.rem(row, 2)
    chip = lax.div(row, 2)
    y = lax.rem(chip, Y)
    x_lo = lax.div(chip, Y)
    z = lax.rem(col, Z)
    x_hi = lax.div(col, Z)
    return row, col, core, x_lo, y, x_hi, z


def send(src, dst, send_sem, recv_sem, row, col):
    copy = pltpu.make_async_remote_copy(
        src_ref=src,
        dst_ref=dst,
        send_sem=send_sem,
        recv_sem=recv_sem,
        device_id=(row, col),
        device_id_type=MESH,
    )
    copy.start()
    return copy


def meet(partners):
    barrier = pltpu.get_barrier_semaphore()
    for partner in partners:
        pl.semaphore_signal(barrier, inc=1, device_id=partner, device_id_type=MESH)
    pl.semaphore_wait(barrier, len(partners))


def near_chips(x_lo, y, core):
    rows = []
    for dx, dy in NEAR:
        there_x = lax.rem(x_lo + dx, 2)
        there_y = lax.rem(y + dy, Y)
        rows.append((there_x * Y + there_y) * 2 + core)
    return rows


class ColGather:
    def __init__(self, mine, gathered, ring_send, ring_recv, far_send, far_recv):
        self.mine = mine
        self.gathered = gathered
        self.ring_send = ring_send
        self.ring_recv = ring_recv
        self.row, self.col, _, _, _, self.x_hi, self.z = where_am_i()
        self.far_send = far_send
        self.far_recv = far_recv
        self.rings = {}

    def block(self, far, z):
        x_hi = 1 - self.x_hi if far else self.x_hi
        return x_hi * Z + lax.rem(z + Z, Z)

    def ring(self, channel, step):
        up = channel in (OWN_UP, FAR_UP)
        far = channel in (FAR_UP, FAR_DOWN)
        shift = 1 if up else -1
        slot = self.block(far, self.z - shift * step)
        src = self.mine if (step == 0 and not far) else self.gathered.at[slot]
        self.rings[channel, step] = send(
            src,
            self.gathered.at[slot],
            self.ring_send.at[channel, step],
            self.ring_recv.at[channel, step],
            self.row,
            self.block(False, self.z + shift),
        )

    def start(self):
        self.exchange = send(
            self.mine,
            self.gathered.at[self.col],
            self.far_send,
            self.far_recv,
            self.row,
            self.block(True, self.z),
        )
        self.ring(OWN_UP, 0)
        self.ring(OWN_DOWN, 0)

    def pass_on(self, channel, step):
        self.rings[channel, step - 1].wait_recv()
        if step < STEPS[channel]:
            self.ring(channel, step)

    def middle(self):
        self.pass_on(OWN_UP, 1)
        self.pass_on(OWN_DOWN, 1)
        self.exchange.wait_recv()
        self.ring(FAR_UP, 0)
        self.ring(FAR_DOWN, 0)
        self.pass_on(OWN_UP, 2)
        self.pass_on(OWN_DOWN, 2)
        self.pass_on(FAR_UP, 1)
        self.pass_on(FAR_DOWN, 1)

    def last(self):
        self.pass_on(OWN_UP, 3)
        self.pass_on(OWN_DOWN, 3)
        self.pass_on(FAR_UP, 2)
        self.pass_on(FAR_DOWN, 2)
        self.pass_on(OWN_UP, 4)
        self.pass_on(FAR_UP, 3)
        self.pass_on(FAR_DOWN, 3)
        self.pass_on(FAR_DOWN, 4)
        self.exchange.wait_send()
        for copy in self.rings.values():
            copy.wait_send()


def gather_kernel(
    x_ref, g_ref, gx_ref, gg_ref,
    ring_send, ring_recv, far_sems, near_send, near_recv, pair_send, pair_recv, own_sems,
):
    row, col, core, x_lo, y, x_hi, z = where_am_i()
    rows = near_chips(x_lo, y, core)
    sibling = row + 1 - 2 * core
    gather = ColGather(x_ref, gx_ref, ring_send, ring_recv, far_sems.at[0], far_sems.at[1])
    meet(
        [(row, gather.block(False, z + 1)), (row, gather.block(False, z - 1)), (row, gather.block(True, z))]
        + [(there, col) for there in rows]
        + [(sibling, col)]
    )
    gather.start()
    own_x = pltpu.make_async_copy(x_ref, gx_ref.at[col], own_sems.at[0])
    own_x.start()
    own_g = pltpu.make_async_copy(g_ref, gg_ref.at[row], own_sems.at[1])
    own_g.start()
    to_pair = [send(g_ref, gg_ref.at[row], pair_send.at[7], pair_recv.at[7], sibling, col)]
    to_near = []
    for i, there in enumerate(rows):
        to_near.append(
            send(g_ref, gg_ref.at[row], near_send.at[i], near_recv.at[i], there, col)
        )
    gather.middle()
    for i, (dx, dy) in enumerate(NEAR):
        from_x = lax.rem(x_lo + dx, 2)
        from_y = lax.rem(y - dy + Y, Y)
        origin = (from_x * Y + from_y) * 2 + core
        to_near[i].wait_recv()
        to_pair.append(
            send(gg_ref.at[origin], gg_ref.at[origin], pair_send.at[i], pair_recv.at[i], sibling, col)
        )
    gather.last()
    for copy in to_pair:
        copy.wait_recv()
    for copy in to_pair + to_near:
        copy.wait_send()
    own_x.wait()
    own_g.wait()


def gather_inputs(x, g):
    return pl.pallas_call(
        gather_kernel,
        out_shape=(
            jax.ShapeDtypeStruct((COL,) + x.shape, x.dtype),
            jax.ShapeDtypeStruct((ROW,) + g.shape, g.dtype),
        ),
        in_specs=[ANY, ANY],
        out_specs=(ANY, ANY),
        scratch_shapes=[
            DMA((4, 4)), DMA((4, 4)), DMA((2,)),
            DMA((7,)), DMA((7,)), DMA((8,)), DMA((8,)), DMA((2,)),
        ],
        compiler_params=pltpu.CompilerParams(collective_id=0, has_side_effects=True),
        name="gather_inputs",
    )(x, g)


def both_kernel(coords, count, tiles, xg, gg, px, pb):
    step = pl.program_id(0)
    dead_row = px.shape[0] - 1

    @pl.when(step == 0)
    def _():
        px[...] = jnp.zeros_like(px)
        pb[...] = jnp.zeros_like(pb)

    @pl.when(step * TILES_AT_ONCE < count[0])
    def _():
        for first in range(0, TILES_AT_ONCE, GROUP):
            places = []
            for j in range(first, first + GROUP):
                slot = step * TILES_AT_ONCE + j
                live = slot < count[0]
                r = coords[2 * slot]
                c = coords[2 * slot + 1]
                tile = tiles[j]
                forward = jnp.dot(tile, xg[c], preferred_element_type=F32)
                back = lax.dot_general(
                    tile, gg[r], (((0,), (0,)), ((), ())), preferred_element_type=F32
                )
                places.append(
                    (jnp.where(live, r, dead_row), jnp.where(live, c, dead_row), forward, back)
                )
            for r, c, forward, back in places:
                px[r] += forward
                pb[c] += back


def one_kernel(coords, count, tiles, xg, px):
    step = pl.program_id(0)
    dead_row = px.shape[0] - 1

    @pl.when(step == 0)
    def _():
        px[...] = jnp.zeros_like(px)

    @pl.when(step * TILES_AT_ONCE < count[0])
    def _():
        for first in range(0, TILES_AT_ONCE, GROUP):
            places = []
            for j in range(first, first + GROUP):
                slot = step * TILES_AT_ONCE + j
                live = slot < count[0]
                r = coords[2 * slot]
                c = coords[2 * slot + 1]
                forward = jnp.dot(tiles[j], xg[c], preferred_element_type=F32)
                places.append((jnp.where(live, r, dead_row), forward))
            for r, forward in places:
                px[r] += forward


def propagate(kernel, coords, count, tiles, sources, name):
    slots, edge, _ = tiles.shape
    whole = lambda shape: pl.BlockSpec(shape, lambda i, *_: (0, 0, 0))
    outs = []
    for source in sources:
        outs.append((source.shape[0] + 1,) + source.shape[1:])
    return pl.pallas_call(
        kernel,
        out_shape=tuple(jax.ShapeDtypeStruct(out, F32) for out in outs),
        grid_spec=pltpu.PrefetchScalarGridSpec(
            num_scalar_prefetch=2,
            grid=(slots // TILES_AT_ONCE,),
            in_specs=[pl.BlockSpec((TILES_AT_ONCE, edge, edge), lambda i, *_: (i, 0, 0))]
            + [whole(source.shape) for source in sources],
            out_specs=tuple(whole(out) for out in outs),
        ),
        name=name,
    )(coords, count, tiles, *sources)


def halves(value):
    high = value.astype(BF16)
    return high, (value - high.astype(F32)).astype(BF16)


def wide_dot(value, weight):
    high, low = halves(value)
    return jnp.dot(high, weight, preferred_element_type=F32) + jnp.dot(
        low, weight, preferred_element_type=F32
    )


class RowReduce:
    def __init__(self, parts, held, pair_in, out_buf, in_buf, pair_send, pair_recv, near_send, near_recv, load_sems):
        self.row, self.col, self.core, self.x_lo, self.y, _, _ = where_am_i()
        self.parts, self.held, self.pair_in = parts, held, pair_in
        self.out_buf, self.in_buf = out_buf, in_buf
        self.pair_send, self.pair_recv = pair_send, pair_recv
        self.near_send, self.near_recv = near_send, near_recv
        self.load_sems = load_sems
        self.sibling = self.row + 1 - 2 * self.core
        self.rows = near_chips(self.x_lo, self.y, self.core)

    def start(self):
        self.pairs, self.loads = [], []
        for i, there in enumerate(self.rows + [self.row]):
            other = there + 1 - 2 * self.core
            self.pairs.append(
                send(
                    self.parts.at[pl.ds(2 * other, 2)], self.pair_in.at[i],
                    self.pair_send.at[i], self.pair_recv.at[i], self.sibling, self.col,
                )
            )
            load = pltpu.make_async_copy(
                self.parts.at[pl.ds(2 * there, 2)], self.held.at[i], self.load_sems.at[i]
            )
            load.start()
            self.loads.append(load)

    def spread(self):
        self.nears = []
        for i, there in enumerate(self.rows):
            self.pairs[i].wait_recv()
            self.loads[i].wait()
            self.out_buf[i] = (self.pair_in[i] + self.held[i]).astype(BF16)
            self.nears.append(
                send(
                    self.out_buf.at[i], self.in_buf.at[i],
                    self.near_send.at[i], self.near_recv.at[i], there, self.col,
                )
            )

    def finish(self):
        self.pairs[7].wait_recv()
        self.loads[7].wait()
        total = self.pair_in[7] + self.held[7]
        for i in range(7):
            self.nears[i].wait_recv()
            total = total + self.in_buf[i].astype(F32)
        return total

    def drain(self):
        for copy in self.pairs + self.nears:
            copy.wait_send()


def row_reduce_scratch(edge, width):
    return [
        pltpu.VMEM((8, 2, edge, width), F32),
        pltpu.VMEM((8, 2, edge, width), F32),
        pltpu.VMEM((7, 2, edge, width), BF16),
        pltpu.VMEM((7, 2, edge, width), BF16),
        DMA((8,)), DMA((8,)), DMA((7,)), DMA((7,)), DMA((8,)),
    ]


def middle_kernel(
    scale,
    px_ref, pb_ref, w1_ref, w2_ref,
    gh_ref, share_ref,
    held, pair_in, out_buf, in_buf, pair_send, pair_recv, near_send, near_recv, load_sems,
    back_out, back_in, back_send, back_recv, back_far_out, back_far_in, back_far_sems,
    h_buf, ring_send, ring_recv, far_sems, own_sem,
    mean_buf, pre_buf, grad_buf, grad_in, grad_send, grad_recv,
):
    row, col, core, x_lo, y, x_hi, z = where_am_i()
    reduce = RowReduce(
        px_ref, held, pair_in, out_buf, in_buf, pair_send, pair_recv, near_send, near_recv, load_sems
    )
    gather = ColGather(h_buf, gh_ref, ring_send, ring_recv, far_sems.at[0], far_sems.at[1])
    far_col = gather.block(True, z)
    up_col = gather.block(False, z + 1)
    down_col = gather.block(False, z - 1)
    others = [lax.rem(row + k, ROW) for k in range(1, ROW)]
    meet([(row, up_col), (row, down_col), (row, far_col)] + [(there, col) for there in others])
    reduce.start()

    nodes = 2 * pb_ref.shape[1]
    width = pb_ref.shape[2]

    def back_part(far, z_to):
        block = gather.block(far, z_to)
        return pb_ref[pl.ds(2 * block, 2)].reshape(nodes, width)

    backs = {}

    def back_step(channel, step):
        up = channel in (OWN_UP, FAR_UP)
        far = channel in (FAR_UP, FAR_DOWN)
        shift = 1 if up else -1
        part = back_part(far, z + shift * (STEPS[channel] - step))
        if step:
            backs[channel, step - 1].wait_recv()
            part = part + back_in[channel, step - 1].astype(F32)
        back_out[channel, step] = part.astype(BF16)
        backs[channel, step] = send(
            back_out.at[channel, step], back_in.at[channel, step],
            back_send.at[channel, step], back_recv.at[channel, step],
            row, up_col if up else down_col,
        )

    for channel in (FAR_DOWN, OWN_UP, FAR_UP, OWN_DOWN):
        back_step(channel, 0)
    reduce.spread()
    for step in (1, 2, 3):
        for channel in (FAR_DOWN, OWN_UP, FAR_UP, OWN_DOWN):
            if step < STEPS[channel]:
                back_step(channel, step)

    def back_total(far):
        total = back_part(far, z)
        for channel in (FAR_UP, FAR_DOWN) if far else (OWN_UP, OWN_DOWN):
            step = STEPS[channel] - 1
            backs[channel, step].wait_recv()
            total = total + back_in[channel, step].astype(F32)
        return total

    back_far_out[...] = back_total(True).astype(BF16)
    back_far = send(
        back_far_out, back_far_in, back_far_sems.at[0], back_far_sems.at[1], row, far_col
    )

    mean = reduce.finish().reshape(nodes, px_ref.shape[2])
    mean_buf[...] = mean
    pre = wide_dot(mean, w1_ref[...])
    pre_buf[...] = pre
    hidden = pre * (1.0 / (1.0 + jnp.exp(-pre)))
    h_buf[...] = wide_dot(hidden, w2_ref[...]).astype(BF16)
    gather.start()
    own = pltpu.make_async_copy(h_buf, gh_ref.at[col], own_sem)
    own.start()

    back_own = back_total(False)
    back_far.wait_recv()
    back = back_own + back_far_in[...].astype(F32)
    hidden_grad = lax.dot_general(
        back, w2_ref[...].astype(F32), (((1,), (1,)), ((), ())),
        precision=HIGHEST, preferred_element_type=F32,
    )
    pre = pre_buf[...]
    sigma = 1.0 / (1.0 + jnp.exp(-pre))
    pre_grad = hidden_grad * (sigma * (1.0 + pre * (1.0 - sigma)))
    contract = (((0,), (0,)), ((), ()))
    second = lax.dot_general(
        pre * sigma, back, contract, precision=HIGHEST, preferred_element_type=F32
    )
    first = lax.dot_general(
        mean_buf[...], pre_grad, contract, precision=HIGHEST, preferred_element_type=F32
    )
    wide = first.shape[0]
    grad_buf[0:wide] = first[:, :width] * scale
    grad_buf[wide : 2 * wide] = first[:, width:] * scale
    grad_buf[2 * wide : 3 * wide] = second * scale
    share = grad_buf.shape[0] // ROW

    gather.middle()
    grads = []
    for k, there in enumerate(others):
        grads.append(
            send(
                grad_buf.at[pl.ds(there * share, share)], grad_in.at[k],
                grad_send.at[k], grad_recv.at[k], there, col,
            )
        )
    gather.last()
    total = grad_buf[pl.ds(row * share, share)]
    for k, copy in enumerate(grads):
        copy.wait_recv()
        total = total + grad_in[k]
    share_ref[...] = total
    reduce.drain()
    for copy in list(backs.values()) + [back_far] + grads:
        copy.wait_send()
    own.wait()


def middle(px, pb, w1, w2, scale):
    edge, wide = px.shape[1:]
    width = pb.shape[2]
    nodes = 2 * edge
    grad_rows = 3 * wide
    share = grad_rows // ROW
    return pl.pallas_call(
        functools.partial(middle_kernel, scale),
        out_shape=(
            jax.ShapeDtypeStruct((COL, nodes, width), BF16),
            jax.ShapeDtypeStruct((share, width), F32),
        ),
        in_specs=[ANY, WHOLE, WHOLE, WHOLE],
        out_specs=(ANY, WHOLE),
        scratch_shapes=row_reduce_scratch(edge, wide)
        + [
            pltpu.VMEM((4, 4, nodes, width), BF16),
            pltpu.VMEM((4, 4, nodes, width), BF16),
            DMA((4, 4)), DMA((4, 4)),
            pltpu.VMEM((nodes, width), BF16),
            pltpu.VMEM((nodes, width), BF16),
            DMA((2,)),
            pltpu.VMEM((nodes, width), BF16),
            DMA((4, 4)), DMA((4, 4)), DMA((2,)), DMA,
            pltpu.VMEM((nodes, wide), F32),
            pltpu.VMEM((nodes, wide), F32),
            pltpu.VMEM((grad_rows, width), F32),
            pltpu.VMEM((ROW - 1, share, width), F32),
            DMA((ROW - 1,)), DMA((ROW - 1,)),
        ],
        compiler_params=pltpu.CompilerParams(collective_id=1, has_side_effects=True),
        name="middle",
    )(px, pb, w1, w2)


def last_kernel(
    ps_ref, share_ref,
    out_ref, grad_ref,
    held, pair_in, out_buf, in_buf, pair_send, pair_recv, near_send, near_recv, load_sems,
    col_in, col_send, col_recv, own_sem, sum_buf, row_send, row_recv,
):
    row, col, core, x_lo, y, x_hi, z = where_am_i()
    reduce = RowReduce(
        ps_ref, held, pair_in, out_buf, in_buf, pair_send, pair_recv, near_send, near_recv, load_sems
    )
    rows = [lax.rem(row + k, ROW) for k in range(1, ROW)]
    cols = [lax.rem(col + k, COL) for k in range(1, COL)]
    meet([(there, col) for there in rows] + [(row, there) for there in cols])
    reduce.start()
    own = pltpu.make_async_copy(share_ref, col_in.at[col], own_sem)
    own.start()
    across = []
    for k, there in enumerate(cols):
        across.append(
            send(share_ref, col_in.at[col], col_send.at[k], col_recv.at[k], row, there)
        )
    reduce.spread()
    own.wait()
    for copy in across:
        copy.wait_recv()
    total = col_in[0]
    for k in range(1, COL):
        total = total + col_in[k]
    sum_buf[...] = total
    share = share_ref.shape[0]
    mine = pl.ds(row * share, share)
    grad_ref[mine] = total
    along = []
    for k, there in enumerate(rows):
        along.append(
            send(sum_buf, grad_ref.at[mine], row_send.at[k], row_recv.at[k], there, col)
        )
    out_ref[...] = reduce.finish().reshape(out_ref.shape).astype(out_ref.dtype)
    for copy in along:
        copy.wait_recv()
    reduce.drain()
    for copy in across + along:
        copy.wait_send()


def last(ps, share):
    edge, width = ps.shape[1:]
    return pl.pallas_call(
        last_kernel,
        out_shape=(
            jax.ShapeDtypeStruct((2 * edge, width), BF16),
            jax.ShapeDtypeStruct((ROW * share.shape[0], width), F32),
        ),
        in_specs=[ANY, WHOLE],
        out_specs=(WHOLE, WHOLE),
        scratch_shapes=row_reduce_scratch(edge, width)
        + [
            pltpu.VMEM((COL,) + share.shape, F32),
            DMA((COL - 1,)), DMA((COL - 1,)), DMA,
            pltpu.VMEM(share.shape, F32),
            DMA((ROW - 1,)), DMA((ROW - 1,)),
        ],
        compiler_params=pltpu.CompilerParams(collective_id=2, has_side_effects=True),
        name="last",
    )(ps, share)


def on_device(
    node_features, tile_values, tile_coords, tile_counts, first_weight, second_weight, out_grad
):
    edge = tile_values.shape[-1]
    slots = tile_values.shape[2]
    tiles = tile_values.reshape(slots, edge, edge)
    coords = tile_coords.reshape(2 * slots)
    count = tile_counts.reshape(1)
    scale = 1.0 / math.sqrt(node_features.shape[0] * ROW * COL)
    gx, gg = gather_inputs(node_features, out_grad)
    px, pb = propagate(
        both_kernel, coords, count, tiles,
        [gx.reshape(-1, edge, gx.shape[-1]), gg.reshape(-1, edge, gg.shape[-1])], "both",
    )
    gh, share = middle(px, pb, first_weight, second_weight, scale)
    (ps,) = propagate(
        one_kernel, coords, count, tiles, [gh.reshape(-1, edge, gh.shape[-1])], "one"
    )
    output, grads = last(ps, share)
    wide = first_weight.shape[0]
    first_grad = jnp.concatenate([grads[:wide], grads[wide : 2 * wide]], axis=1)
    return (output, first_grad, grads[2 * wide :])


def solution(mesh):
    return jax.shard_map(
        on_device,
        mesh=mesh,
        in_specs=(
            P(("row", "col"), None),
            P("row", "col", None, None, None),
            P("row", "col", None, None),
            P("row", "col"),
            P(),
            P(),
            P(("row", "col"), None),
        ),
        out_specs=(P(("row", "col"), None), P(), P()),
        check_vma=False,
    )
```

time: 900 us -> 132 us (0.15)
  waiting for transfers between devices: 688 us -> 0 us
  matrix products: 147 us -> 0 us
  Pallas kernels: 0 us -> 125 us
  local copies, waits for them, and re-layouts: 47.9 us -> 4.68 us
  between operations: 14.8 us -> 1.3 us
    reduce_scatter x3 -> x0, waiting for transfers between devices: 264 us -> none  [the longest x1 131 us: on_device(): lax.psum_scatter(grad_part, 'col', scatter_dimension=0, tiled=True)]
    psum x1 -> x0, waiting for transfers between devices: 255 us -> none  [on_device(): first_grad = lax.psum(first_local, ('row', 'col'))]
    all_gather x3 -> x0, waiting for transfers between devices: 169 us -> none  [the longest x1 86.8 us: on_device(): gathered_x = lax.all_gather(node_features, 'col', axis=0, tiled=True)]
    dot_general x29 -> x0, matrix products: 147 us -> none  [the longest x12 99.3 us: add_group(): jnp.einsum('tr,taw->raw', select, products, precision=HIGHEST)]
    pallas_call x0 -> x5, Pallas kernels: none -> 125 us  [the longest x1 46 us: middle(): pl.pallas_call(functools.partial(middle_kernel, scale), out_shape=(jax.Sh...]
    gather x12 -> x0, local copies, waits for them, and re-layouts: 26.2 us -> none  [add_group(): picked = jnp.take(source, group_source, axis=0)]
    while x3 -> x0, local copies, waits for them, and re-layouts: 17.3 us -> none  [tile_sum(): lax.scan(add_group, start_sum, (grouped_tiles, grouped_dest, grouped_sour...]
  transfers between devices with their start and end apart: 7 -> 0, of which waited for: 7 -> 0; matrix products, arithmetic and copies ran while one was open for 13% -> 0% of each run, Pallas kernels for 0% -> 0%
where the time goes in v1:
time: 132 us
  Pallas kernels  125 us (95%)
  local copies, waits for them, and re-layouts  4.68 us (4%)
    pallas_call x1, Pallas kernels, middle(): pl.pallas_call(functools.partial(middle_kernel, scale), out_shape=(jax.Sh...  46 us
    pallas_call x1, Pallas kernels, gather_inputs(): pl.pallas_call(gather_kernel, out_shape=(jax.ShapeDtypeStruct((COL,) + x....  34.9 us
    pallas_call x1, Pallas kernels, last(): pl.pallas_call(last_kernel, out_shape=(jax.ShapeDtypeStruct((2 * edge, wi...  26.2 us
    pallas_call x2, Pallas kernels, propagate(): pl.pallas_call(kernel, out_shape=tuple((jax.ShapeDtypeStruct(out, F32) fo...  18 us

profile of v1, /device:TPU:1, one launch (start us, length us, event | category | flops | bytes accessed | tf_op | source)
XLA Modules:
  0.0 131.8 jit_solution(10723961829630234679)
XLA Ops:
  1.3 0.8 copy.10
  2.1 0.7 reshape.24.coords
  2.8 34.9 %gather_inputs.1 = (bf16[16,256,256]{2,1,0:T(8,128)(2,1)}, bf16[16,256,128]{2,1,0:T(8,128)(2,1)}) custom-call(bf16[256,256]{1,0:T(8,128)(2,1)} %x_ref.1, bf16[256,128]{1,0:T(8,128)(2,1)} %g_ref.1), custom_call_target="tpu_custom_call" | custom-call | tf_op jit(solution)/shard_map/gather_inputs/pallas_call | solution.py:187
  37.6 10.4 %both.1 = (f32[33,128,256]{2,1,0:T(8,128)}, f32[33,128,128]{2,1,0:T(8,128)}) custom-call(s32[256]{0:T(256)} %reshape.24.coords, s32[1]{0:T(128)} %bitcast.7.count, bf16[128,128,128]{2,1,0:T(8,128)(2,1)} %bitcast.9, bf16[32,128,256]{2,1,0:T(8,128)(2,1)} %bitcast.11, bf16[32,128,128]{2,1,0:T(8,128)(2,1)} %bitcast.13), custom_call_target="tpu_custom_call" | custom-call | tf_op jit(solution)/shard_map/both/pallas_call | solution.py:264
  48.1 46.0 %middle.1 = (bf16[16,256,128]{2,1,0:T(8,128)(2,1)}, f32[48,128]{1,0:T(8,128)}) custom-call(f32[33,128,256]{2,1,0:T(8,128)} %get-tuple-element.13.px_ref, f32[33,128,128]{2,1,0:T(8,128)} %get-tuple-element.14.pb_ref, bf16[256,256]{1,0:T(8,128)(2,1)} %w1_ref.1, bf16[256,128]{1,0:T(8,128)(2,1)} %w2_ref.1), custom_call_target="tpu_custom_call" | custom-call | tf_op jit(solution)/shard_map/middle/pallas_call | solution.py:480
  94.1 7.6 %one.1.ps_ref = f32[33,128,128]{2,1,0:T(8,128)} custom-call(s32[256]{0:T(256)} %reshape.24.coords, s32[1]{0:T(128)} %bitcast.8.count, bf16[128,128,128]{2,1,0:T(8,128)(2,1)} %bitcast.10, bf16[32,128,128]{2,1,0:T(8,128)(2,1)} %bitcast.12), custom_call_target="tpu_custom_call" | custom-call | tf_op jit(solution)/shard_map/one/pallas_call | solution.py:264
  101.7 26.2 %last.1 = (bf16[256,128]{1,0:T(8,128)(2,1)}, f32[768,128]{1,0:T(8,128)}) custom-call(f32[33,128,128]{2,1,0:T(8,128)} %one.1.ps_ref, f32[48,128]{1,0:T(8,128)} %get-tuple-element.16.share_ref), custom_call_target="tpu_custom_call" | custom-call | tf_op jit(solution)/shard_map/last/pallas_call | solution.py:556
  127.9 1.7 %fusion = (f32[256,128]{1,0:T(8,128)}, f32[256,128]{1,0:T(8,128)S(1)}, f32[256,128]{1,0:T(8,128)S(1)}) fusion(f32[768,128]{1,0:T(8,128)} %get-tuple-element.18), kind=kLoop, calls=%fused_computation.1 | loop fusion | bytes 786432 | tf_op jit(solution)/shard_map/slice | solution.py:597
  129.6 0.7 pad_maximum_fusion
  130.3 1.5 %copy.13 = bf16[256,128]{1,0:T(8,128)(2,1)} copy(bf16[256,128]{1,0:T(8,128)(2,1)} %get-tuple-element.25) | data formatting | bytes 131072

commit v2 on v1

--- a/solution.py
+++ b/solution.py
@@ -78,77 +78,85 @@
         self.row, self.col, _, _, _, self.x_hi, self.z = where_am_i()
         self.far_send = far_send
         self.far_recv = far_recv
+        self.pieces = far_send.shape[0]
+        self.size = mine.shape[0] // self.pieces
         self.rings = {}
+        self.exchange = []
 
     def block(self, far, z):
         x_hi = 1 - self.x_hi if far else self.x_hi
         return x_hi * Z + lax.rem(z + Z, Z)
 
-    def ring(self, channel, step):
+    def ring(self, channel, step, piece):
         up = channel in (OWN_UP, FAR_UP)
         far = channel in (FAR_UP, FAR_DOWN)
         shift = 1 if up else -1
         slot = self.block(far, self.z - shift * step)
-        src = self.mine if (step == 0 and not far) else self.gathered.at[slot]
-        self.rings[channel, step] = send(
-            src,
-            self.gathered.at[slot],
-            self.ring_send.at[channel, step],
-            self.ring_recv.at[channel, step],
+        rows = pl.ds(piece * self.size, self.size)
+        there = self.gathered.at[slot, rows]
+        self.rings[channel, step, piece] = send(
+            self.mine.at[rows] if (step == 0 and not far) else there,
+            there,
+            self.ring_send.at[channel, step, piece],
+            self.ring_recv.at[channel, step, piece],
             self.row,
             self.block(False, self.z + shift),
         )
 
     def start(self):
-        self.exchange = send(
-            self.mine,
-            self.gathered.at[self.col],
-            self.far_send,
-            self.far_recv,
-            self.row,
-            self.block(True, self.z),
-        )
-        self.ring(OWN_UP, 0)
-        self.ring(OWN_DOWN, 0)
-
-    def pass_on(self, channel, step):
-        self.rings[channel, step - 1].wait_recv()
+        for piece in range(self.pieces):
+            rows = pl.ds(piece * self.size, self.size)
+            self.exchange.append(
+                send(
+                    self.mine.at[rows],
+                    self.gathered.at[self.col, rows],
+                    self.far_send.at[piece],
+                    self.far_recv.at[piece],
+                    self.row,
+                    self.block(True, self.z),
+                )
+            )
+            self.ring(OWN_UP, 0, piece)
+            self.ring(OWN_DOWN, 0, piece)
+
+    def pass_on(self, channel, step, piece):
+        if step <= STEPS[channel]:
+            self.rings[channel, step - 1, piece].wait_recv()
         if step < STEPS[channel]:
-            self.ring(channel, step)
-
-    def middle(self):
-        self.pass_on(OWN_UP, 1)
-        self.pass_on(OWN_DOWN, 1)
-        self.exchange.wait_recv()
-        self.ring(FAR_UP, 0)
-        self.ring(FAR_DOWN, 0)
-        self.pass_on(OWN_UP, 2)
-        self.pass_on(OWN_DOWN, 2)
-        self.pass_on(FAR_UP, 1)
-        self.pass_on(FAR_DOWN, 1)
-
-    def last(self):
-        self.pass_on(OWN_UP, 3)
-        self.pass_on(OWN_DOWN, 3)
-        self.pass_on(FAR_UP, 2)
-        self.pass_on(FAR_DOWN, 2)
-        self.pass_on(OWN_UP, 4)
-        self.pass_on(FAR_UP, 3)
-        self.pass_on(FAR_DOWN, 3)
-        self.pass_on(FAR_DOWN, 4)
-        self.exchange.wait_send()
-        for copy in self.rings.values():
+            self.ring(channel, step, piece)
+
+    def phase(self, number):
+        for piece in range(self.pieces):
+            self.pass_on(OWN_UP, number + 1, piece)
+            self.pass_on(OWN_DOWN, number + 1, piece)
+            if number == 0:
+                self.exchange[piece].wait_recv()
+                self.ring(FAR_UP, 0, piece)
+                self.ring(FAR_DOWN, 0, piece)
+            else:
+                self.pass_on(FAR_UP, number, piece)
+                self.pass_on(FAR_DOWN, number, piece)
+
+    def drain(self):
+        for copy in self.exchange + list(self.rings.values()):
             copy.wait_send()
+
+
+PHASES = 5
+
+
+def gather_sems(pieces):
+    return [DMA((4, 4, pieces)), DMA((4, 4, pieces)), DMA((pieces,)), DMA((pieces,))]
 
 
 def gather_kernel(
     x_ref, g_ref, gx_ref, gg_ref,
-    ring_send, ring_recv, far_sems, near_send, near_recv, pair_send, pair_recv, own_sems,
+    ring_send, ring_recv, far_send, far_recv, near_send, near_recv, pair_send, pair_recv, own_sems,
 ):
     row, col, core, x_lo, y, x_hi, z = where_am_i()
     rows = near_chips(x_lo, y, core)
     sibling = row + 1 - 2 * core
-    gather = ColGather(x_ref, gx_ref, ring_send, ring_recv, far_sems.at[0], far_sems.at[1])
+    gather = ColGather(x_ref, gx_ref, ring_send, ring_recv, far_send, far_recv)
     meet(
         [(row, gather.block(False, z + 1)), (row, gather.block(False, z - 1)), (row, gather.block(True, z))]
         + [(there, col) for there in rows]
@@ -165,7 +173,8 @@
         to_near.append(
             send(g_ref, gg_ref.at[row], near_send.at[i], near_recv.at[i], there, col)
         )
-    gather.middle()
+    gather.phase(0)
+    gather.phase(1)
     for i, (dx, dy) in enumerate(NEAR):
         from_x = lax.rem(x_lo + dx, 2)
         from_y = lax.rem(y - dy + Y, Y)
@@ -174,7 +183,9 @@
         to_pair.append(
             send(gg_ref.at[origin], gg_ref.at[origin], pair_send.at[i], pair_recv.at[i], sibling, col)
         )
-    gather.last()
+    for number in range(2, PHASES):
+        gather.phase(number)
+    gather.drain()
     for copy in to_pair:
         copy.wait_recv()
     for copy in to_pair + to_near:
@@ -193,7 +204,7 @@
         in_specs=[ANY, ANY],
         out_specs=(ANY, ANY),
         scratch_shapes=[
-            DMA((4, 4)), DMA((4, 4)), DMA((2,)),
+            *gather_sems(2),
             DMA((7,)), DMA((7,)), DMA((8,)), DMA((8,)), DMA((2,)),
         ],
         compiler_params=pltpu.CompilerParams(collective_id=0, has_side_effects=True),
@@ -217,8 +228,8 @@
             for j in range(first, first + GROUP):
                 slot = step * TILES_AT_ONCE + j
                 live = slot < count[0]
-                r = coords[2 * slot]
-                c = coords[2 * slot + 1]
+                r = coords[0, slot]
+                c = coords[1, slot]
                 tile = tiles[j]
                 forward = jnp.dot(tile, xg[c], preferred_element_type=F32)
                 back = lax.dot_general(
@@ -247,8 +258,8 @@
             for j in range(first, first + GROUP):
                 slot = step * TILES_AT_ONCE + j
                 live = slot < count[0]
-                r = coords[2 * slot]
-                c = coords[2 * slot + 1]
+                r = coords[0, slot]
+                c = coords[1, slot]
                 forward = jnp.dot(tiles[j], xg[c], preferred_element_type=F32)
                 places.append((jnp.where(live, r, dead_row), forward))
             for r, forward in places:
@@ -357,19 +368,19 @@
     gh_ref, share_ref,
     held, pair_in, out_buf, in_buf, pair_send, pair_recv, near_send, near_recv, load_sems,
     back_out, back_in, back_send, back_recv, back_far_out, back_far_in, back_far_sems,
-    h_buf, ring_send, ring_recv, far_sems, own_sem,
-    mean_buf, pre_buf, grad_buf, grad_in, grad_send, grad_recv,
+    h_buf, ring_send, ring_recv, far_send, far_recv, own_sem,
+    mean_buf, pre_buf, grad_buf, grad_pair, pair_sems, half_buf, grad_in, grad_send, grad_recv,
 ):
     row, col, core, x_lo, y, x_hi, z = where_am_i()
     reduce = RowReduce(
         px_ref, held, pair_in, out_buf, in_buf, pair_send, pair_recv, near_send, near_recv, load_sems
     )
-    gather = ColGather(h_buf, gh_ref, ring_send, ring_recv, far_sems.at[0], far_sems.at[1])
+    gather = ColGather(h_buf, gh_ref, ring_send, ring_recv, far_send, far_recv)
     far_col = gather.block(True, z)
     up_col = gather.block(False, z + 1)
     down_col = gather.block(False, z - 1)
-    others = [lax.rem(row + k, ROW) for k in range(1, ROW)]
-    meet([(row, up_col), (row, down_col), (row, far_col)] + [(there, col) for there in others])
+    partners = [(there, col) for there in [reduce.sibling] + reduce.rows]
+    meet([(row, up_col), (row, down_col), (row, far_col)] + partners)
     reduce.start()
 
     nodes = 2 * pb_ref.shape[1]
@@ -412,11 +423,6 @@
             total = total + back_in[channel, step].astype(F32)
         return total
 
-    back_far_out[...] = back_total(True).astype(BF16)
-    back_far = send(
-        back_far_out, back_far_in, back_far_sems.at[0], back_far_sems.at[1], row, far_col
-    )
-
     mean = reduce.finish().reshape(nodes, px_ref.shape[2])
     mean_buf[...] = mean
     pre = wide_dot(mean, w1_ref[...])
@@ -427,7 +433,12 @@
     own = pltpu.make_async_copy(h_buf, gh_ref.at[col], own_sem)
     own.start()
 
+    back_far_out[...] = back_total(True).astype(BF16)
+    back_far = send(
+        back_far_out, back_far_in, back_far_sems.at[0], back_far_sems.at[1], row, far_col
+    )
     back_own = back_total(False)
+    gather.phase(0)
     back_far.wait_recv()
     back = back_own + back_far_in[...].astype(F32)
     hidden_grad = lax.dot_general(
@@ -438,6 +449,7 @@
     sigma = 1.0 / (1.0 + jnp.exp(-pre))
     pre_grad = hidden_grad * (sigma * (1.0 + pre * (1.0 - sigma)))
     contract = (((0,), (0,)), ((), ()))
+    gather.phase(1)
     second = lax.dot_general(
         pre * sigma, back, contract, precision=HIGHEST, preferred_element_type=F32
     )
@@ -448,25 +460,33 @@
     grad_buf[0:wide] = first[:, :width] * scale
     grad_buf[wide : 2 * wide] = first[:, width:] * scale
     grad_buf[2 * wide : 3 * wide] = second * scale
-    share = grad_buf.shape[0] // ROW
-
-    gather.middle()
+    half = grad_buf.shape[0] // 2
+    share = half // CHIPS
+    pair = send(
+        grad_buf.at[pl.ds((1 - core) * half, half)], grad_pair,
+        pair_sems.at[0], pair_sems.at[1], reduce.sibling, col,
+    )
+    gather.phase(2)
+    pair.wait_recv()
+    half_buf[...] = grad_buf[pl.ds(core * half, half)] + grad_pair[...]
     grads = []
-    for k, there in enumerate(others):
+    for i, there in enumerate(reduce.rows):
         grads.append(
             send(
-                grad_buf.at[pl.ds(there * share, share)], grad_in.at[k],
-                grad_send.at[k], grad_recv.at[k], there, col,
+                half_buf.at[pl.ds(lax.div(there, 2) * share, share)], grad_in.at[i],
+                grad_send.at[i], grad_recv.at[i], there, col,
             )
         )
-    gather.last()
-    total = grad_buf[pl.ds(row * share, share)]
-    for k, copy in enumerate(grads):
+    gather.phase(3)
+    gather.phase(4)
+    total = half_buf[pl.ds(lax.div(row, 2) * share, share)]
+    for i, copy in enumerate(grads):
         copy.wait_recv()
-        total = total + grad_in[k]
-    share_ref[...] = total
+        total = total + grad_in[i]
+    share_ref[...] = total.astype(BF16)
     reduce.drain()
-    for copy in list(backs.values()) + [back_far] + grads:
+    gather.drain()
+    for copy in list(backs.values()) + [back_far, pair] + grads:
         copy.wait_send()
     own.wait()
 
@@ -481,7 +501,7 @@
         functools.partial(middle_kernel, scale),
         out_shape=(
             jax.ShapeDtypeStruct((COL, nodes, width), BF16),
-            jax.ShapeDtypeStruct((share, width), F32),
+            jax.ShapeDtypeStruct((share, width), BF16),
         ),
         in_specs=[ANY, WHOLE, WHOLE, WHOLE],
         out_specs=(ANY, WHOLE),
@@ -494,12 +514,15 @@
             pltpu.VMEM((nodes, width), BF16),
             DMA((2,)),
             pltpu.VMEM((nodes, width), BF16),
-            DMA((4, 4)), DMA((4, 4)), DMA((2,)), DMA,
+            *gather_sems(2), DMA,
             pltpu.VMEM((nodes, wide), F32),
             pltpu.VMEM((nodes, wide), F32),
             pltpu.VMEM((grad_rows, width), F32),
-            pltpu.VMEM((ROW - 1, share, width), F32),
-            DMA((ROW - 1,)), DMA((ROW - 1,)),
+            pltpu.VMEM((grad_rows // 2, width), F32),
+            DMA((2,)),
+            pltpu.VMEM((grad_rows // 2, width), F32),
+            pltpu.VMEM((CHIPS - 1, share, width), F32),
+            DMA((CHIPS - 1,)), DMA((CHIPS - 1,)),
         ],
         compiler_params=pltpu.CompilerParams(collective_id=1, has_side_effects=True),
         name="middle",
@@ -510,44 +533,59 @@
     ps_ref, share_ref,
     out_ref, grad_ref,
     held, pair_in, out_buf, in_buf, pair_send, pair_recv, near_send, near_recv, load_sems,
-    col_in, col_send, col_recv, own_sem, sum_buf, row_send, row_recv,
+    col_in, ring_send, ring_recv, far_send, far_recv, own_sem,
+    sum_buf, row_send, row_recv, twin_send, twin_recv,
 ):
     row, col, core, x_lo, y, x_hi, z = where_am_i()
     reduce = RowReduce(
         ps_ref, held, pair_in, out_buf, in_buf, pair_send, pair_recv, near_send, near_recv, load_sems
     )
-    rows = [lax.rem(row + k, ROW) for k in range(1, ROW)]
-    cols = [lax.rem(col + k, COL) for k in range(1, COL)]
-    meet([(there, col) for there in rows] + [(row, there) for there in cols])
+    gather = ColGather(share_ref, col_in, ring_send, ring_recv, far_send, far_recv)
+    ring = [gather.block(False, z + 1), gather.block(False, z - 1), gather.block(True, z)]
+    sibling = reduce.sibling
+    meet([(there, col) for there in [sibling] + reduce.rows] + [(row, there) for there in ring])
+    gather.start()
     reduce.start()
     own = pltpu.make_async_copy(share_ref, col_in.at[col], own_sem)
     own.start()
-    across = []
-    for k, there in enumerate(cols):
-        across.append(
-            send(share_ref, col_in.at[col], col_send.at[k], col_recv.at[k], row, there)
-        )
     reduce.spread()
+    for number in range(PHASES):
+        gather.phase(number)
     own.wait()
-    for copy in across:
-        copy.wait_recv()
-    total = col_in[0]
+    total = col_in[0].astype(F32)
     for k in range(1, COL):
-        total = total + col_in[k]
+        total = total + col_in[k].astype(F32)
     sum_buf[...] = total
     share = share_ref.shape[0]
-    mine = pl.ds(row * share, share)
+
+    def place(chip):
+        return pl.ds((core * CHIPS + chip) * share, share)
+
+    mine = place(lax.div(row, 2))
     grad_ref[mine] = total
     along = []
-    for k, there in enumerate(rows):
+    for i, there in enumerate(reduce.rows):
         along.append(
-            send(sum_buf, grad_ref.at[mine], row_send.at[k], row_recv.at[k], there, col)
+            send(sum_buf, grad_ref.at[mine], row_send.at[i], row_recv.at[i], there, col)
         )
-    out_ref[...] = reduce.finish().reshape(out_ref.shape).astype(out_ref.dtype)
-    for copy in along:
+    twins = [send(sum_buf, grad_ref.at[mine], twin_send.at[7], twin_recv.at[7], sibling, col)]
+    out_ref[...] = reduce.finish().reshape(out_ref.shape)
+    for i, (dx, dy) in enumerate(NEAR):
+        from_x = lax.rem(x_lo + dx, 2)
+        from_y = lax.rem(y - dy + Y, Y)
+        along[i].wait_recv()
+        theirs = place(from_x * Y + from_y)
+        twins.append(
+            send(
+                grad_ref.at[theirs], grad_ref.at[theirs],
+                twin_send.at[i], twin_recv.at[i], sibling, col,
+            )
+        )
+    for copy in twins:
         copy.wait_recv()
     reduce.drain()
-    for copy in across + along:
+    gather.drain()
+    for copy in along + twins:
         copy.wait_send()
 
 
@@ -556,21 +594,44 @@
     return pl.pallas_call(
         last_kernel,
         out_shape=(
-            jax.ShapeDtypeStruct((2 * edge, width), BF16),
+            jax.ShapeDtypeStruct((2 * edge, width), F32),
             jax.ShapeDtypeStruct((ROW * share.shape[0], width), F32),
         ),
         in_specs=[ANY, WHOLE],
         out_specs=(WHOLE, WHOLE),
         scratch_shapes=row_reduce_scratch(edge, width)
         + [
-            pltpu.VMEM((COL,) + share.shape, F32),
-            DMA((COL - 1,)), DMA((COL - 1,)), DMA,
+            pltpu.VMEM((COL,) + share.shape, BF16),
+            *gather_sems(1), DMA,
             pltpu.VMEM(share.shape, F32),
-            DMA((ROW - 1,)), DMA((ROW - 1,)),
+            DMA((7,)), DMA((7,)), DMA((8,)), DMA((8,)),
         ],
         compiler_params=pltpu.CompilerParams(collective_id=2, has_side_effects=True),
         name="last",
     )(ps, share)
+
+
+def arrange_kernel(out_ref, grad_ref, output_ref, first_ref, second_ref):
+    wide = first_ref.shape[0]
+    width = second_ref.shape[1]
+    output_ref[...] = out_ref[...].astype(BF16)
+    first_ref[:, :width] = grad_ref[:wide]
+    first_ref[:, width:] = grad_ref[wide : 2 * wide]
+    second_ref[...] = grad_ref[2 * wide :]
+
+
+def arrange(out, grads, wide):
+    return pl.pallas_call(
+        arrange_kernel,
+        out_shape=(
+            jax.ShapeDtypeStruct(out.shape, BF16),
+            jax.ShapeDtypeStruct((wide, 2 * grads.shape[1]), F32),
+            jax.ShapeDtypeStruct((wide, grads.shape[1]), F32),
+        ),
+        in_specs=[WHOLE, WHOLE],
+        out_specs=(WHOLE, WHOLE, WHOLE),
+        name="arrange",
+    )(out, grads)
 
 
 def on_device(
@@ -579,7 +640,7 @@
     edge = tile_values.shape[-1]
     slots = tile_values.shape[2]
     tiles = tile_values.reshape(slots, edge, edge)
-    coords = tile_coords.reshape(2 * slots)
+    coords = tile_coords.reshape(slots, 2).T
     count = tile_counts.reshape(1)
     scale = 1.0 / math.sqrt(node_features.shape[0] * ROW * COL)
     gx, gg = gather_inputs(node_features, out_grad)
@@ -591,10 +652,8 @@
     (ps,) = propagate(
         one_kernel, coords, count, tiles, [gh.reshape(-1, edge, gh.shape[-1])], "one"
     )
-    output, grads = last(ps, share)
-    wide = first_weight.shape[0]
-    first_grad = jnp.concatenate([grads[:wide], grads[wide : 2 * wide]], axis=1)
-    return (output, first_grad, grads[2 * wide :])
+    out, grads = last(ps, share)
+    return arrange(out, grads, first_weight.shape[0])
 
 
 def solution(mesh):

time: 132 us -> 129 us (0.977)
  local copies, waits for them, and re-layouts: 4.68 us -> 0 us
  Pallas kernels: 125 us -> 127 us
    pallas_call x1, Pallas kernels: 46 us -> 42.1 us  [middle(): pl.pallas_call(functools.partial(middle_kernel, scale), out_shape=(jax.Sh...]
    pallas_call x1, Pallas kernels: 26.2 us -> 29.6 us  [last(): pl.pallas_call(last_kernel, out_shape=(jax.ShapeDtypeStruct((2 * edge, wi...]
    unnamed x2 -> x0, local copies, waits for them, and re-layouts: 2.26 us -> none
    pallas_call x0 -> x1, Pallas kernels: none -> 1.85 us  [arrange(): pl.pallas_call(arrange_kernel, out_shape=(jax.ShapeDtypeStruct(out.shape,...]
    pallas_call x2, Pallas kernels: 18 us -> 19.8 us  [propagate(): pl.pallas_call(kernel, out_shape=tuple((jax.ShapeDtypeStruct(out, F32) fo...]
    slice x1 -> x0, local copies, waits for them, and re-layouts: 1.71 us -> none  [on_device(): return (output, first_grad, grads[2 * wide:])]
where the time goes in v2:
time: 129 us; the launch traced here: 128 us
  Pallas kernels  127 us (98%)
  between operations  1.3 us (1%)
    pallas_call x1, Pallas kernels, middle(): pl.pallas_call(functools.partial(middle_kernel, scale), out_shape=(jax.Sh...  42.1 us
    pallas_call x1, Pallas kernels, gather_inputs(): pl.pallas_call(gather_kernel, out_shape=(jax.ShapeDtypeStruct((COL,) + x....  33.9 us
    pallas_call x1, Pallas kernels, last(): pl.pallas_call(last_kernel, out_shape=(jax.ShapeDtypeStruct((2 * edge, wi...  29.6 us
    pallas_call x2, Pallas kernels, propagate(): pl.pallas_call(kernel, out_shape=tuple((jax.ShapeDtypeStruct(out, F32) fo...  19.8 us

profile of v2, /device:TPU:1, one launch (start us, length us, event | category | flops | bytes accessed | tf_op | source)
XLA Modules:
  0.0 128.5 jit_solution(5131910607814336575)
XLA Ops:
  1.3 33.9 %gather_inputs.1 = (bf16[16,256,256]{2,1,0:T(8,128)(2,1)}, bf16[16,256,128]{2,1,0:T(8,128)(2,1)}) custom-call(bf16[256,256]{1,0:T(8,128)(2,1)} %x_ref.1, bf16[256,128]{1,0:T(8,128)(2,1)} %g_ref.1), custom_call_target="tpu_custom_call" | custom-call | tf_op jit(solution)/shard_map/gather_inputs/pallas_call | solution.py:198
  35.1 11.6 %both.1 = (f32[33,128,256]{2,1,0:T(8,128)}, f32[33,128,128]{2,1,0:T(8,128)}) custom-call(s32[2,128]{1,0:T(2,128)} %bitcast.15, s32[1]{0:T(128)} %bitcast.8.count, bf16[128,128,128]{2,1,0:T(8,128)(2,1)} %bitcast.10, bf16[32,128,256]{2,1,0:T(8,128)(2,1)} %bitcast.12, bf16[32,128,128]{2,1,0:T(8,128)(2,1)} %bitcast.14), custom_call_target="tpu_custom_call" | custom-call | tf_op jit(solution)/shard_map/both/pallas_call | solution.py:275
  46.7 42.1 %middle.1 = (bf16[16,256,128]{2,1,0:T(8,128)(2,1)}, bf16[48,128]{1,0:T(8,128)(2,1)}) custom-call(f32[33,128,256]{2,1,0:T(8,128)} %get-tuple-element.13.px_ref, f32[33,128,128]{2,1,0:T(8,128)} %get-tuple-element.14.pb_ref, bf16[256,256]{1,0:T(8,128)(2,1)} %w1_ref.1, bf16[256,128]{1,0:T(8,128)(2,1)} %w2_ref.1), custom_call_target="tpu_custom_call" | custom-call | tf_op jit(solution)/shard_map/middle/pallas_call | solution.py:500
  88.8 8.2 %one.1.ps_ref = f32[33,128,128]{2,1,0:T(8,128)} custom-call(s32[2,128]{1,0:T(2,128)} %bitcast.16, s32[1]{0:T(128)} %bitcast.9.count, bf16[128,128,128]{2,1,0:T(8,128)(2,1)} %bitcast.11, bf16[32,128,128]{2,1,0:T(8,128)(2,1)} %bitcast.13), custom_call_target="tpu_custom_call" | custom-call | tf_op jit(solution)/shard_map/one/pallas_call | solution.py:275
  97.0 29.6 %last.1 = (f32[256,128]{1,0:T(8,128)}, f32[768,128]{1,0:T(8,128)}) custom-call(f32[33,128,128]{2,1,0:T(8,128)} %one.1.ps_ref, bf16[48,128]{1,0:T(8,128)(2,1)} %get-tuple-element.16.share_ref), custom_call_target="tpu_custom_call" | custom-call | tf_op jit(solution)/shard_map/last/pallas_call | solution.py:594
  126.6 1.9 %arrange.1 = (bf16[256,128]{1,0:T(8,128)(2,1)}, f32[256,256]{1,0:T(8,128)}, f32[256,128]{1,0:T(8,128)}) custom-call(f32[256,128]{1,0:T(8,128)} %get-tuple-element.17.out_ref, f32[768,128]{1,0:T(8,128)} %get-tuple-element.18.grad_ref), custom_call_target="tpu_custom_call" | custom-call | tf_op jit(solution)/shard_map/arrange/pallas_call | solution.py:624

commit v3 on v2

--- a/solution.py
+++ b/solution.py
@@ -25,6 +25,7 @@
 OWN_UP, OWN_DOWN, FAR_UP, FAR_DOWN = 0, 1, 2, 3
 STEPS = (4, 3, 3, 4)
 TILES_AT_ONCE = 16
+SCOPED = 24 * 2**20
 GROUP = 4
 
 
@@ -207,7 +208,7 @@
             *gather_sems(2),
             DMA((7,)), DMA((7,)), DMA((8,)), DMA((8,)), DMA((2,)),
         ],
-        compiler_params=pltpu.CompilerParams(collective_id=0, has_side_effects=True),
+        compiler_params=pltpu.CompilerParams(collective_id=0, has_side_effects=True, vmem_limit_bytes=SCOPED),
         name="gather_inputs",
     )(x, g)
 
@@ -282,6 +283,7 @@
             + [whole(source.shape) for source in sources],
             out_specs=tuple(whole(out) for out in outs),
         ),
+        compiler_params=pltpu.CompilerParams(vmem_limit_bytes=SCOPED),
         name=name,
     )(coords, count, tiles, *sources)
 
@@ -524,7 +526,7 @@
             pltpu.VMEM((CHIPS - 1, share, width), F32),
             DMA((CHIPS - 1,)), DMA((CHIPS - 1,)),
         ],
-        compiler_params=pltpu.CompilerParams(collective_id=1, has_side_effects=True),
+        compiler_params=pltpu.CompilerParams(collective_id=1, has_side_effects=True, vmem_limit_bytes=SCOPED),
         name="middle",
     )(px, pb, w1, w2)
 
@@ -533,25 +535,28 @@
     ps_ref, share_ref,
     out_ref, grad_ref,
     held, pair_in, out_buf, in_buf, pair_send, pair_recv, near_send, near_recv, load_sems,
-    col_in, ring_send, ring_recv, far_send, far_recv, own_sem,
+    col_in, col_send, col_recv, own_sem,
     sum_buf, row_send, row_recv, twin_send, twin_recv,
 ):
     row, col, core, x_lo, y, x_hi, z = where_am_i()
     reduce = RowReduce(
         ps_ref, held, pair_in, out_buf, in_buf, pair_send, pair_recv, near_send, near_recv, load_sems
     )
-    gather = ColGather(share_ref, col_in, ring_send, ring_recv, far_send, far_recv)
-    ring = [gather.block(False, z + 1), gather.block(False, z - 1), gather.block(True, z)]
+    cols = [lax.rem(col + k, COL) for k in range(1, COL)]
     sibling = reduce.sibling
-    meet([(there, col) for there in [sibling] + reduce.rows] + [(row, there) for there in ring])
-    gather.start()
+    meet([(there, col) for there in [sibling] + reduce.rows] + [(row, there) for there in cols])
+    across = []
+    for k, there in enumerate(cols):
+        across.append(
+            send(share_ref, col_in.at[col], col_send.at[k], col_recv.at[k], row, there)
+        )
     reduce.start()
     own = pltpu.make_async_copy(share_ref, col_in.at[col], own_sem)
     own.start()
     reduce.spread()
-    for number in range(PHASES):
-        gather.phase(number)
     own.wait()
+    for copy in across:
+        copy.wait_recv()
     total = col_in[0].astype(F32)
     for k in range(1, COL):
         total = total + col_in[k].astype(F32)
@@ -584,8 +589,7 @@
     for copy in twins:
         copy.wait_recv()
     reduce.drain()
-    gather.drain()
-    for copy in along + twins:
+    for copy in across + along + twins:
         copy.wait_send()
 
 
@@ -602,11 +606,11 @@
         scratch_shapes=row_reduce_scratch(edge, width)
         + [
             pltpu.VMEM((COL,) + share.shape, BF16),
-            *gather_sems(1), DMA,
+            DMA((COL - 1,)), DMA((COL - 1,)), DMA,
             pltpu.VMEM(share.shape, F32),
             DMA((7,)), DMA((7,)), DMA((8,)), DMA((8,)),
         ],
-        compiler_params=pltpu.CompilerParams(collective_id=2, has_side_effects=True),
+        compiler_params=pltpu.CompilerParams(collective_id=2, has_side_effects=True, vmem_limit_bytes=SCOPED),
         name="last",
     )(ps, share)
 
@@ -630,8 +634,13 @@
         ),
         in_specs=[WHOLE, WHOLE],
         out_specs=(WHOLE, WHOLE, WHOLE),
+        compiler_params=pltpu.CompilerParams(vmem_limit_bytes=SCOPED),
         name="arrange",
     )(out, grads)
+
+
+def in_hbm(array):
+    return pltpu.with_memory_space_constraint(array, pltpu.HBM)
 
 
 def on_device(
@@ -643,9 +652,9 @@
     coords = tile_coords.reshape(slots, 2).T
     count = tile_counts.reshape(1)
     scale = 1.0 / math.sqrt(node_features.shape[0] * ROW * COL)
-    gx, gg = gather_inputs(node_features, out_grad)
+    gx, gg = gather_inputs(in_hbm(node_features), in_hbm(out_grad))
     px, pb = propagate(
-        both_kernel, coords, count, tiles,
+        both_kernel, coords, count, in_hbm(tiles),
         [gx.reshape(-1, edge, gx.shape[-1]), gg.reshape(-1, edge, gg.shape[-1])], "both",
     )
     gh, share = middle(px, pb, first_weight, second_weight, scale)

time: 129 us -> 106 us (0.82)
  Pallas kernels: 127 us -> 104 us
    pallas_call x2, Pallas kernels: 19.8 us -> 8.07 us  [propagate(): pl.pallas_call(kernel, out_shape=tuple((jax.ShapeDtypeStruct(out, F32) fo...]
    pallas_call x1, Pallas kernels: 29.6 us -> 23.1 us  [last(): pl.pallas_call(last_kernel, out_shape=(jax.ShapeDtypeStruct((2 * edge, wi...]
    pallas_call x1, Pallas kernels: 42.1 us -> 38.6 us  [middle(): pl.pallas_call(functools.partial(middle_kernel, scale), out_shape=(jax.Sh...]
where the time goes in v3:
time: 106 us
  Pallas kernels  104 us (98%)
  between operations  1.33 us (1%)
    pallas_call x1, Pallas kernels, middle(): pl.pallas_call(functools.partial(middle_kernel, scale), out_shape=(jax.Sh...  38.6 us
    pallas_call x1, Pallas kernels, gather_inputs(): pl.pallas_call(gather_kernel, out_shape=(jax.ShapeDtypeStruct((COL,) + x....  33.1 us
    pallas_call x1, Pallas kernels, last(): pl.pallas_call(last_kernel, out_shape=(jax.ShapeDtypeStruct((2 * edge, wi...  23.1 us
    pallas_call x2, Pallas kernels, propagate(): pl.pallas_call(kernel, out_shape=tuple((jax.ShapeDtypeStruct(out, F32) fo...  8.07 us

profile of v3, /device:TPU:1, one launch (start us, length us, event | category | flops | bytes accessed | tf_op | source)
XLA Modules:
  0.0 105.6 jit_solution(13689362293453338159)
XLA Ops:
  1.3 33.1 %gather_inputs.1 = (bf16[16,256,256]{2,1,0:T(8,128)(2,1)S(1)}, bf16[16,256,128]{2,1,0:T(8,128)(2,1)S(1)}) custom-call(bf16[256,256]{1,0:T(8,128)(2,1)} %x_ref.1, bf16[256,128]{1,0:T(8,128)(2,1)} %g_ref.1), custom_call_target="tpu_custom_call" | custom-call | tf_op jit(solution)/shard_map/gather_inputs/pallas_call | solution.py:199
  34.4 0.0 copy-start.3
  34.4 0.7 copy-done.3
  35.1 0.0 copy-start.1
  35.1 0.0 copy-start.2
  35.1 6.5 %both.1 = (f32[33,128,256]{2,1,0:T(8,128)S(1)}, f32[33,128,128]{2,1,0:T(8,128)S(1)}) custom-call(s32[2,128]{1,0:T(2,128)S(1)} %bitcast.15, s32[1]{0:T(128)} %bitcast.8.count, bf16[128,128,128]{2,1,0:T(8,128)(2,1)} %bitcast.10, bf16[32,128,256]{2,1,0:T(8,128)(2,1)S(1)} %bitcast.12, bf16[32,128,128]{2,1,0:T(8,128)(2,1)S(1)} %bitcast.14), custom_call_target="tpu_custom_call" | custom-call | tf_op jit(solution)/shard_map/both/pallas_call | solution.py:276
  41.6 0.0 copy-done.1
  41.6 0.0 copy-done.2
  41.6 0.0 copy-start
  41.6 38.6 %middle.1 = (bf16[16,256,128]{2,1,0:T(8,128)(2,1)S(1)}, bf16[48,128]{1,0:T(8,128)(2,1)S(1)}) custom-call(f32[33,128,256]{2,1,0:T(8,128)S(1)} %get-tuple-element.13.px_ref, f32[33,128,128]{2,1,0:T(8,128)S(1)} %get-tuple-element.14.pb_ref, bf16[256,256]{1,0:T(8,128)(2,1)S(1)} %copy-done.1, bf16[256,128]{1,0:T(8,128)(2,1)S(1)} %copy-done.2), custom_call_target="tpu_custom_call" | custom-call | tf_op jit(solution)/shard_map/middle/pallas_call | solution.py:502
  80.2 0.0 copy-done
  80.2 1.5 %one.1.ps_ref = f32[33,128,128]{2,1,0:T(8,128)S(1)} custom-call(s32[2,128]{1,0:T(2,128)S(1)} %bitcast.16, s32[1]{0:T(128)} %bitcast.9.count, bf16[128,128,128]{2,1,0:T(8,128)(2,1)S(1)} %bitcast.11, bf16[32,128,128]{2,1,0:T(8,128)(2,1)S(1)} %bitcast.13), custom_call_target="tpu_custom_call" | custom-call | tf_op jit(solution)/shard_map/one/pallas_call | solution.py:276
  81.8 23.1 %last.1 = (f32[256,128]{1,0:T(8,128)S(1)}, f32[768,128]{1,0:T(8,128)S(1)}) custom-call(f32[33,128,128]{2,1,0:T(8,128)S(1)} %one.1.ps_ref, bf16[48,128]{1,0:T(8,128)(2,1)S(1)} %get-tuple-element.16.share_ref), custom_call_target="tpu_custom_call" | custom-call | tf_op jit(solution)/shard_map/last/pallas_call | solution.py:598
  104.8 0.8 arrange.1
Async XLA Ops:
  34.4 0.7 copy-start.3
  35.1 6.6 %copy-start.1 = (bf16[256,256]{1,0:T(8,128)(2,1)S(1)}, bf16[256,256]{1,0:T(8,128)(2,1)}, u32[]{:S(2)}) copy-start(bf16[256,256]{1,0:T(8,128)(2,1)} %w1_ref.1) | copy-start | bytes 393220
  35.1 6.6 %copy-start.2 = (bf16[256,128]{1,0:T(8,128)(2,1)S(1)}, bf16[256,128]{1,0:T(8,128)(2,1)}, u32[]{:S(2)}) copy-start(bf16[256,128]{1,0:T(8,128)(2,1)} %w2_ref.1) | copy-start | bytes 196612
  41.6 38.6 %copy-start = (bf16[1,1,128,128,128]{4,3,2,1,0:T(8,128)(2,1)S(1)}, bf16[1,1,128,128,128]{4,3,2,1,0:T(8,128)(2,1)}, u32[]{:S(2)}) copy-start(bf16[1,1,128,128,128]{4,3,2,1,0:T(8,128)(2,1)} %param.8) | copy-start | bytes 12582916

commit v4 on v3

--- a/solution.py
+++ b/solution.py
@@ -8,7 +8,6 @@
 from jax.experimental.pallas import tpu as pltpu
 from jax.sharding import PartitionSpec as P
 
-HIGHEST = lax.Precision.HIGHEST
 MESH = pl.DeviceIdType.MESH
 ANY = pl.BlockSpec(memory_space=pl.ANY)
 WHOLE = pl.BlockSpec(memory_space=pltpu.VMEM)
@@ -94,14 +93,17 @@
         shift = 1 if up else -1
         slot = self.block(far, self.z - shift * step)
         rows = pl.ds(piece * self.size, self.size)
+        row, col = self.row, self.block(False, self.z + shift)
+        if far and step == 0:
+            slot, col = self.block(False, self.z - shift), self.block(True, self.z)
         there = self.gathered.at[slot, rows]
         self.rings[channel, step, piece] = send(
             self.mine.at[rows] if (step == 0 and not far) else there,
             there,
             self.ring_send.at[channel, step, piece],
             self.ring_recv.at[channel, step, piece],
-            self.row,
-            self.block(False, self.z + shift),
+            row,
+            col,
         )
 
     def start(self):
@@ -129,16 +131,18 @@
     def phase(self, number):
         for piece in range(self.pieces):
             self.pass_on(OWN_UP, number + 1, piece)
+            if number == 0:
+                self.ring(FAR_UP, 0, piece)
             self.pass_on(OWN_DOWN, number + 1, piece)
             if number == 0:
-                self.exchange[piece].wait_recv()
-                self.ring(FAR_UP, 0, piece)
                 self.ring(FAR_DOWN, 0, piece)
             else:
                 self.pass_on(FAR_UP, number, piece)
                 self.pass_on(FAR_DOWN, number, piece)
 
     def drain(self):
+        for copy in self.exchange:
+            copy.wait_recv()
         for copy in self.exchange + list(self.rings.values()):
             copy.wait_send()
 
@@ -151,10 +155,12 @@
 
 
 def gather_kernel(
-    x_ref, g_ref, gx_ref, gg_ref,
+    x_ref, g_ref, tiles_ref, gx_ref, gg_ref, near_tiles_ref,
     ring_send, ring_recv, far_send, far_recv, near_send, near_recv, pair_send, pair_recv, own_sems,
 ):
     row, col, core, x_lo, y, x_hi, z = where_am_i()
+    own_tiles = pltpu.make_async_copy(tiles_ref, near_tiles_ref, own_sems.at[2])
+    own_tiles.start()
     rows = near_chips(x_lo, y, core)
     sibling = row + 1 - 2 * core
     gather = ColGather(x_ref, gx_ref, ring_send, ring_recv, far_send, far_recv)
@@ -193,24 +199,26 @@
         copy.wait_send()
     own_x.wait()
     own_g.wait()
-
-
-def gather_inputs(x, g):
+    own_tiles.wait()
+
+
+def gather_inputs(x, g, tiles):
     return pl.pallas_call(
         gather_kernel,
         out_shape=(
             jax.ShapeDtypeStruct((COL,) + x.shape, x.dtype),
             jax.ShapeDtypeStruct((ROW,) + g.shape, g.dtype),
+            jax.ShapeDtypeStruct(tiles.shape, tiles.dtype),
         ),
-        in_specs=[ANY, ANY],
-        out_specs=(ANY, ANY),
+        in_specs=[ANY, ANY, ANY],
+        out_specs=(ANY, ANY, ANY),
         scratch_shapes=[
             *gather_sems(2),
-            DMA((7,)), DMA((7,)), DMA((8,)), DMA((8,)), DMA((2,)),
+            DMA((7,)), DMA((7,)), DMA((8,)), DMA((8,)), DMA((3,)),
         ],
         compiler_params=pltpu.CompilerParams(collective_id=0, has_side_effects=True, vmem_limit_bytes=SCOPED),
         name="gather_inputs",
-    )(x, g)
+    )(x, g, tiles)
 
 
 def both_kernel(coords, count, tiles, xg, gg, px, pb):
@@ -300,6 +308,15 @@
     )
 
 
+def split_dot(left, right, contract):
+    left_high, left_low = halves(left)
+    right_high, right_low = halves(right)
+    total = lax.dot_general(left_high, right_high, contract, preferred_element_type=F32)
+    total += lax.dot_general(left_high, right_low, contract, preferred_element_type=F32)
+    total += lax.dot_general(left_low, right_high, contract, preferred_element_type=F32)
+    return total
+
+
 class RowReduce:
     def __init__(self, parts, held, pair_in, out_buf, in_buf, pair_send, pair_recv, near_send, near_recv, load_sems):
         self.row, self.col, self.core, self.x_lo, self.y, _, _ = where_am_i()
@@ -426,6 +443,10 @@
         return total
 
     mean = reduce.finish().reshape(nodes, px_ref.shape[2])
+    back_far_out[...] = back_total(True).astype(BF16)
+    back_far = send(
+        back_far_out, back_far_in, back_far_sems.at[0], back_far_sems.at[1], row, far_col
+    )
     mean_buf[...] = mean
     pre = wide_dot(mean, w1_ref[...])
     pre_buf[...] = pre
@@ -435,29 +456,22 @@
     own = pltpu.make_async_copy(h_buf, gh_ref.at[col], own_sem)
     own.start()
 
-    back_far_out[...] = back_total(True).astype(BF16)
-    back_far = send(
-        back_far_out, back_far_in, back_far_sems.at[0], back_far_sems.at[1], row, far_col
-    )
     back_own = back_total(False)
     gather.phase(0)
     back_far.wait_recv()
     back = back_own + back_far_in[...].astype(F32)
+    back_high, back_low = halves(back)
+    across = (((1,), (1,)), ((), ()))
     hidden_grad = lax.dot_general(
-        back, w2_ref[...].astype(F32), (((1,), (1,)), ((), ())),
-        precision=HIGHEST, preferred_element_type=F32,
-    )
+        back_high, w2_ref[...], across, preferred_element_type=F32
+    ) + lax.dot_general(back_low, w2_ref[...], across, preferred_element_type=F32)
     pre = pre_buf[...]
     sigma = 1.0 / (1.0 + jnp.exp(-pre))
     pre_grad = hidden_grad * (sigma * (1.0 + pre * (1.0 - sigma)))
     contract = (((0,), (0,)), ((), ()))
     gather.phase(1)
-    second = lax.dot_general(
-        pre * sigma, back, contract, precision=HIGHEST, preferred_element_type=F32
-    )
-    first = lax.dot_general(
-        mean_buf[...], pre_grad, contract, precision=HIGHEST, preferred_element_type=F32
-    )
+    second = split_dot(pre * sigma, back, contract)
+    first = split_dot(mean_buf[...], pre_grad, contract)
     wide = first.shape[0]
     grad_buf[0:wide] = first[:, :width] * scale
     grad_buf[wide : 2 * wide] = first[:, width:] * scale
@@ -649,12 +663,12 @@
     edge = tile_values.shape[-1]
     slots = tile_values.shape[2]
     tiles = tile_values.reshape(slots, edge, edge)
-    coords = tile_coords.reshape(slots, 2).T
+    coords = in_hbm(tile_coords.reshape(slots, 2).T)
     count = tile_counts.reshape(1)
     scale = 1.0 / math.sqrt(node_features.shape[0] * ROW * COL)
-    gx, gg = gather_inputs(in_hbm(node_features), in_hbm(out_grad))
+    gx, gg, tiles = gather_inputs(in_hbm(node_features), in_hbm(out_grad), in_hbm(tiles))
     px, pb = propagate(
-        both_kernel, coords, count, in_hbm(tiles),
+        both_kernel, coords, count, tiles,
         [gx.reshape(-1, edge, gx.shape[-1]), gg.reshape(-1, edge, gg.shape[-1])], "both",
     )
     gh, share = middle(px, pb, first_weight, second_weight, scale)

time: 106 us -> 107 us (level)
    pallas_call x1, Pallas kernels: 33.1 us -> 36.4 us  [gather_inputs(): pl.pallas_call(gather_kernel, out_shape=(jax.ShapeDtypeStruct((COL,) + x....]
    pallas_call x1, Pallas kernels: 38.6 us -> 36.3 us  [middle(): pl.pallas_call(functools.partial(middle_kernel, scale), out_shape=(jax.Sh...]
    pallas_call x2, Pallas kernels: 8.07 us -> 9.63 us  [propagate(): pl.pallas_call(kernel, out_shape=tuple((jax.ShapeDtypeStruct(out, F32) fo...]
where the time goes in v4:
time: 107 us
  Pallas kernels  105 us (98%)
  between operations  1.35 us (1%)
    pallas_call x1, Pallas kernels, gather_inputs(): pl.pallas_call(gather_kernel, out_shape=(jax.ShapeDtypeStruct((COL,) + x....  36.4 us
    pallas_call x1, Pallas kernels, middle(): pl.pallas_call(functools.partial(middle_kernel, scale), out_shape=(jax.Sh...  36.3 us
    pallas_call x1, Pallas kernels, last(): pl.pallas_call(last_kernel, out_shape=(jax.ShapeDtypeStruct((2 * edge, wi...  22.1 us
    pallas_call x2, Pallas kernels, propagate(): pl.pallas_call(kernel, out_shape=tuple((jax.ShapeDtypeStruct(out, F32) fo...  9.63 us

profile of v4, /device:TPU:1, one launch (start us, length us, event | category | flops | bytes accessed | tf_op | source)
XLA Modules:
  0.0 106.5 jit_solution(16102767984242266619)
XLA Ops:
  1.3 36.4 %gather_inputs.1 = (bf16[16,256,256]{2,1,0:T(8,128)(2,1)S(1)}, bf16[16,256,128]{2,1,0:T(8,128)(2,1)S(1)}, bf16[128,128,128]{2,1,0:T(8,128)(2,1)S(1)}) custom-call(bf16[256,256]{1,0:T(8,128)(2,1)} %x_ref.1, bf16[256,128]{1,0:T(8,128)(2,1)} %g_ref.1, bf16[128,128,128]{2,1,0:T(8,128)(2,1)} %bitcast.13), custom_call_target="tpu_custom_call" | custom-call | tf_op jit(solution)/shard_map/gather_inputs/pallas_call | solution.py:206
  37.7 0.0 copy-start
  37.7 0.0 copy-start.1
  37.7 6.2 %both.1 = (f32[33,128,256]{2,1,0:T(8,128)S(1)}, f32[33,128,128]{2,1,0:T(8,128)S(1)}) custom-call(s32[2,128]{1,0:T(2,128)} %bitcast.14, s32[1]{0:T(128)} %bitcast.8.count, bf16[128,128,128]{2,1,0:T(8,128)(2,1)S(1)} %get-tuple-element.12.tiles, bf16[32,128,256]{2,1,0:T(8,128)(2,1)S(1)} %bitcast.10, bf16[32,128,128]{2,1,0:T(8,128)(2,1)S(1)} %bitcast.12), custom_call_target="tpu_custom_call" | custom-call | tf_op jit(solution)/shard_map/both/pallas_call | solution.py:284
  43.9 0.0 copy-done
  43.9 0.0 copy-done.1
  43.9 36.3 %middle.1 = (bf16[16,256,128]{2,1,0:T(8,128)(2,1)S(1)}, bf16[48,128]{1,0:T(8,128)(2,1)S(1)}) custom-call(f32[33,128,256]{2,1,0:T(8,128)S(1)} %get-tuple-element.15.px_ref, f32[33,128,128]{2,1,0:T(8,128)S(1)} %get-tuple-element.16.pb_ref, bf16[256,256]{1,0:T(8,128)(2,1)S(1)} %copy-done, bf16[256,128]{1,0:T(8,128)(2,1)S(1)} %copy-done.1), custom_call_target="tpu_custom_call" | custom-call | tf_op jit(solution)/shard_map/middle/pallas_call | solution.py:516
  80.2 3.5 %one.1.ps_ref = f32[33,128,128]{2,1,0:T(8,128)S(1)} custom-call(s32[2,128]{1,0:T(2,128)} %bitcast.15, s32[1]{0:T(128)} %bitcast.9.count, bf16[128,128,128]{2,1,0:T(8,128)(2,1)S(1)} %get-tuple-element.12.tiles, bf16[32,128,128]{2,1,0:T(8,128)(2,1)S(1)} %bitcast.11), custom_call_target="tpu_custom_call" | custom-call | tf_op jit(solution)/shard_map/one/pallas_call | solution.py:284
  83.6 22.1 %last.1 = (f32[256,128]{1,0:T(8,128)S(1)}, f32[768,128]{1,0:T(8,128)S(1)}) custom-call(f32[33,128,128]{2,1,0:T(8,128)S(1)} %one.1.ps_ref, bf16[48,128]{1,0:T(8,128)(2,1)S(1)} %get-tuple-element.18.share_ref), custom_call_target="tpu_custom_call" | custom-call | tf_op jit(solution)/shard_map/last/pallas_call | solution.py:612
  105.7 0.8 arrange.1
Async XLA Ops:
  37.7 6.2 %copy-start = (bf16[256,256]{1,0:T(8,128)(2,1)S(1)}, bf16[256,256]{1,0:T(8,128)(2,1)}, u32[]{:S(2)}) copy-start(bf16[256,256]{1,0:T(8,128)(2,1)} %w1_ref.1) | copy-start | bytes 393220
  37.7 6.2 %copy-start.1 = (bf16[256,128]{1,0:T(8,128)(2,1)S(1)}, bf16[256,128]{1,0:T(8,128)(2,1)}, u32[]{:S(2)}) copy-start(bf16[256,128]{1,0:T(8,128)(2,1)} %w2_ref.1) | copy-start | bytes 196612

commit v5 on v4

--- a/solution.py
+++ b/solution.py
@@ -93,17 +93,14 @@
         shift = 1 if up else -1
         slot = self.block(far, self.z - shift * step)
         rows = pl.ds(piece * self.size, self.size)
-        row, col = self.row, self.block(False, self.z + shift)
-        if far and step == 0:
-            slot, col = self.block(False, self.z - shift), self.block(True, self.z)
         there = self.gathered.at[slot, rows]
         self.rings[channel, step, piece] = send(
             self.mine.at[rows] if (step == 0 and not far) else there,
             there,
             self.ring_send.at[channel, step, piece],
             self.ring_recv.at[channel, step, piece],
-            row,
-            col,
+            self.row,
+            self.block(False, self.z + shift),
         )
 
     def start(self):
@@ -131,18 +128,16 @@
     def phase(self, number):
         for piece in range(self.pieces):
             self.pass_on(OWN_UP, number + 1, piece)
-            if number == 0:
-                self.ring(FAR_UP, 0, piece)
             self.pass_on(OWN_DOWN, number + 1, piece)
             if number == 0:
+                self.exchange[piece].wait_recv()
+                self.ring(FAR_UP, 0, piece)
                 self.ring(FAR_DOWN, 0, piece)
             else:
                 self.pass_on(FAR_UP, number, piece)
                 self.pass_on(FAR_DOWN, number, piece)
 
     def drain(self):
-        for copy in self.exchange:
-            copy.wait_recv()
         for copy in self.exchange + list(self.rings.values()):
             copy.wait_send()
 
@@ -159,8 +154,6 @@
     ring_send, ring_recv, far_send, far_recv, near_send, near_recv, pair_send, pair_recv, own_sems,
 ):
     row, col, core, x_lo, y, x_hi, z = where_am_i()
-    own_tiles = pltpu.make_async_copy(tiles_ref, near_tiles_ref, own_sems.at[2])
-    own_tiles.start()
     rows = near_chips(x_lo, y, core)
     sibling = row + 1 - 2 * core
     gather = ColGather(x_ref, gx_ref, ring_send, ring_recv, far_send, far_recv)
@@ -180,6 +173,8 @@
         to_near.append(
             send(g_ref, gg_ref.at[row], near_send.at[i], near_recv.at[i], there, col)
         )
+    own_tiles = pltpu.make_async_copy(tiles_ref, near_tiles_ref, own_sems.at[2])
+    own_tiles.start()
     gather.phase(0)
     gather.phase(1)
     for i, (dx, dy) in enumerate(NEAR):

time: 107 us -> 104 us (0.972)
  Pallas kernels: 105 us -> 103 us
    pallas_call x1, Pallas kernels: 36.3 us -> 40.8 us  [middle(): pl.pallas_call(functools.partial(middle_kernel, scale), out_shape=(jax.Sh...]
    pallas_call x2, Pallas kernels: 9.63 us -> 5.18 us  [propagate(): pl.pallas_call(kernel, out_shape=tuple((jax.ShapeDtypeStruct(out, F32) fo...]
    pallas_call x1, Pallas kernels: 36.4 us -> 33.1 us  [gather_inputs(): pl.pallas_call(gather_kernel, out_shape=(jax.ShapeDtypeStruct((COL,) + x....]
where the time goes in v5:
time: 104 us
  Pallas kernels  103 us (99%)
  between operations  1.35 us (1%)
    pallas_call x1, Pallas kernels, middle(): pl.pallas_call(functools.partial(middle_kernel, scale), out_shape=(jax.Sh...  40.8 us
    pallas_call x1, Pallas kernels, gather_inputs(): pl.pallas_call(gather_kernel, out_shape=(jax.ShapeDtypeStruct((COL,) + x....  33.1 us
    pallas_call x1, Pallas kernels, last(): pl.pallas_call(last_kernel, out_shape=(jax.ShapeDtypeStruct((2 * edge, wi...  22.9 us
    pallas_call x2, Pallas kernels, propagate(): pl.pallas_call(kernel, out_shape=tuple((jax.ShapeDtypeStruct(out, F32) fo...  5.18 us

profile of v5, /device:TPU:1, one launch (start us, length us, event | category | flops | bytes accessed | tf_op | source)
XLA Modules:
  0.0 104.1 jit_solution(14997132310632710416)
XLA Ops:
  1.3 33.1 %gather_inputs.1 = (bf16[16,256,256]{2,1,0:T(8,128)(2,1)S(1)}, bf16[16,256,128]{2,1,0:T(8,128)(2,1)S(1)}, bf16[128,128,128]{2,1,0:T(8,128)(2,1)S(1)}) custom-call(bf16[256,256]{1,0:T(8,128)(2,1)} %x_ref.1, bf16[256,128]{1,0:T(8,128)(2,1)} %g_ref.1, bf16[128,128,128]{2,1,0:T(8,128)(2,1)} %bitcast.13), custom_call_target="tpu_custom_call" | custom-call | tf_op jit(solution)/shard_map/gather_inputs/pallas_call | solution.py:201
  34.4 0.0 copy-start
  34.4 0.0 copy-start.1
  34.4 3.2 %both.1 = (f32[33,128,256]{2,1,0:T(8,128)S(1)}, f32[33,128,128]{2,1,0:T(8,128)S(1)}) custom-call(s32[2,128]{1,0:T(2,128)} %bitcast.14, s32[1]{0:T(128)} %bitcast.8.count, bf16[128,128,128]{2,1,0:T(8,128)(2,1)S(1)} %get-tuple-element.12.tiles, bf16[32,128,256]{2,1,0:T(8,128)(2,1)S(1)} %bitcast.10, bf16[32,128,128]{2,1,0:T(8,128)(2,1)S(1)} %bitcast.12), custom_call_target="tpu_custom_call" | custom-call | tf_op jit(solution)/shard_map/both/pallas_call | solution.py:279
  37.6 0.0 copy-done
  37.7 0.0 copy-done.1
  37.7 40.8 %middle.1 = (bf16[16,256,128]{2,1,0:T(8,128)(2,1)S(1)}, bf16[48,128]{1,0:T(8,128)(2,1)S(1)}) custom-call(f32[33,128,256]{2,1,0:T(8,128)S(1)} %get-tuple-element.15.px_ref, f32[33,128,128]{2,1,0:T(8,128)S(1)} %get-tuple-element.16.pb_ref, bf16[256,256]{1,0:T(8,128)(2,1)S(1)} %copy-done, bf16[256,128]{1,0:T(8,128)(2,1)S(1)} %copy-done.1), custom_call_target="tpu_custom_call" | custom-call | tf_op jit(solution)/shard_map/middle/pallas_call | solution.py:511
  78.4 1.9 %one.1.ps_ref = f32[33,128,128]{2,1,0:T(8,128)S(1)} custom-call(s32[2,128]{1,0:T(2,128)} %bitcast.15, s32[1]{0:T(128)} %bitcast.9.count, bf16[128,128,128]{2,1,0:T(8,128)(2,1)S(1)} %get-tuple-element.12.tiles, bf16[32,128,128]{2,1,0:T(8,128)(2,1)S(1)} %bitcast.11), custom_call_target="tpu_custom_call" | custom-call | tf_op jit(solution)/shard_map/one/pallas_call | solution.py:279
  80.4 22.9 %last.1 = (f32[256,128]{1,0:T(8,128)S(1)}, f32[768,128]{1,0:T(8,128)S(1)}) custom-call(f32[33,128,128]{2,1,0:T(8,128)S(1)} %one.1.ps_ref, bf16[48,128]{1,0:T(8,128)(2,1)S(1)} %get-tuple-element.18.share_ref), custom_call_target="tpu_custom_call" | custom-call | tf_op jit(solution)/shard_map/last/pallas_call | solution.py:607
  103.3 0.8 arrange.1
Async XLA Ops:
  34.4 3.3 %copy-start = (bf16[256,256]{1,0:T(8,128)(2,1)S(1)}, bf16[256,256]{1,0:T(8,128)(2,1)}, u32[]{:S(2)}) copy-start(bf16[256,256]{1,0:T(8,128)(2,1)} %w1_ref.1) | copy-start | bytes 393220
  34.4 3.3 %copy-start.1 = (bf16[256,128]{1,0:T(8,128)(2,1)S(1)}, bf16[256,128]{1,0:T(8,128)(2,1)}, u32[]{:S(2)}) copy-start(bf16[256,128]{1,0:T(8,128)(2,1)} %w2_ref.1) | copy-start | bytes 196612

commit v6 on v5

--- a/solution.py
+++ b/solution.py
@@ -208,7 +208,7 @@
         in_specs=[ANY, ANY, ANY],
         out_specs=(ANY, ANY, ANY),
         scratch_shapes=[
-            *gather_sems(2),
+            *gather_sems(4),
             DMA((7,)), DMA((7,)), DMA((8,)), DMA((8,)), DMA((3,)),
         ],
         compiler_params=pltpu.CompilerParams(collective_id=0, has_side_effects=True, vmem_limit_bytes=SCOPED),
@@ -525,7 +525,7 @@
             pltpu.VMEM((nodes, width), BF16),
             DMA((2,)),
             pltpu.VMEM((nodes, width), BF16),
-            *gather_sems(2), DMA,
+            *gather_sems(4), DMA,
             pltpu.VMEM((nodes, wide), F32),
             pltpu.VMEM((nodes, wide), F32),
             pltpu.VMEM((grad_rows, width), F32),

time: 104 us -> 105 us (level)
    pallas_call x1, Pallas kernels: 40.8 us -> 42.5 us  [middle(): pl.pallas_call(functools.partial(middle_kernel, scale), out_shape=(jax.Sh...]
where the time goes in v6:
time: 105 us
  Pallas kernels  104 us (99%)
  between operations  1.35 us (1%)
    pallas_call x1, Pallas kernels, middle(): pl.pallas_call(functools.partial(middle_kernel, scale), out_shape=(jax.Sh...  42.5 us
    pallas_call x1, Pallas kernels, gather_inputs(): pl.pallas_call(gather_kernel, out_shape=(jax.ShapeDtypeStruct((COL,) + x....  33 us
    pallas_call x1, Pallas kernels, last(): pl.pallas_call(last_kernel, out_shape=(jax.ShapeDtypeStruct((2 * edge, wi...  23.1 us
    pallas_call x2, Pallas kernels, propagate(): pl.pallas_call(kernel, out_shape=tuple((jax.ShapeDtypeStruct(out, F32) fo...  4.3 us

profile of v6, /device:TPU:1, one launch (start us, length us, event | category | flops | bytes accessed | tf_op | source)
XLA Modules:
  0.0 105.1 jit_solution(4259681185253523169)
XLA Ops:
  1.3 33.0 %gather_inputs.1 = (bf16[16,256,256]{2,1,0:T(8,128)(2,1)S(1)}, bf16[16,256,128]{2,1,0:T(8,128)(2,1)S(1)}, bf16[128,128,128]{2,1,0:T(8,128)(2,1)S(1)}) custom-call(bf16[256,256]{1,0:T(8,128)(2,1)} %x_ref.1, bf16[256,128]{1,0:T(8,128)(2,1)} %g_ref.1, bf16[128,128,128]{2,1,0:T(8,128)(2,1)} %bitcast.13), custom_call_target="tpu_custom_call" | custom-call | tf_op jit(solution)/shard_map/gather_inputs/pallas_call | solution.py:201
  34.3 0.0 copy-start
  34.3 0.0 copy-start.1
  34.4 2.6 %both.1 = (f32[33,128,256]{2,1,0:T(8,128)S(1)}, f32[33,128,128]{2,1,0:T(8,128)S(1)}) custom-call(s32[2,128]{1,0:T(2,128)} %bitcast.14, s32[1]{0:T(128)} %bitcast.8.count, bf16[128,128,128]{2,1,0:T(8,128)(2,1)S(1)} %get-tuple-element.12.tiles, bf16[32,128,256]{2,1,0:T(8,128)(2,1)S(1)} %bitcast.10, bf16[32,128,128]{2,1,0:T(8,128)(2,1)S(1)} %bitcast.12), custom_call_target="tpu_custom_call" | custom-call | tf_op jit(solution)/shard_map/both/pallas_call | solution.py:279
  37.0 0.0 copy-done
  37.0 0.0 copy-done.1
  37.0 42.5 %middle.1 = (bf16[16,256,128]{2,1,0:T(8,128)(2,1)S(1)}, bf16[48,128]{1,0:T(8,128)(2,1)S(1)}) custom-call(f32[33,128,256]{2,1,0:T(8,128)S(1)} %get-tuple-element.15.px_ref, f32[33,128,128]{2,1,0:T(8,128)S(1)} %get-tuple-element.16.pb_ref, bf16[256,256]{1,0:T(8,128)(2,1)S(1)} %copy-done, bf16[256,128]{1,0:T(8,128)(2,1)S(1)} %copy-done.1), custom_call_target="tpu_custom_call" | custom-call | tf_op jit(solution)/shard_map/middle/pallas_call | solution.py:511
  79.5 1.7 %one.1.ps_ref = f32[33,128,128]{2,1,0:T(8,128)S(1)} custom-call(s32[2,128]{1,0:T(2,128)} %bitcast.15, s32[1]{0:T(128)} %bitcast.9.count, bf16[128,128,128]{2,1,0:T(8,128)(2,1)S(1)} %get-tuple-element.12.tiles, bf16[32,128,128]{2,1,0:T(8,128)(2,1)S(1)} %bitcast.11), custom_call_target="tpu_custom_call" | custom-call | tf_op jit(solution)/shard_map/one/pallas_call | solution.py:279
  81.2 23.1 %last.1 = (f32[256,128]{1,0:T(8,128)S(1)}, f32[768,128]{1,0:T(8,128)S(1)}) custom-call(f32[33,128,128]{2,1,0:T(8,128)S(1)} %one.1.ps_ref, bf16[48,128]{1,0:T(8,128)(2,1)S(1)} %get-tuple-element.18.share_ref), custom_call_target="tpu_custom_call" | custom-call | tf_op jit(solution)/shard_map/last/pallas_call | solution.py:607
  104.3 0.8 arrange.1
Async XLA Ops:
  34.3 2.7 %copy-start = (bf16[256,256]{1,0:T(8,128)(2,1)S(1)}, bf16[256,256]{1,0:T(8,128)(2,1)}, u32[]{:S(2)}) copy-start(bf16[256,256]{1,0:T(8,128)(2,1)} %w1_ref.1) | copy-start | bytes 393220
  34.3 2.7 %copy-start.1 = (bf16[256,128]{1,0:T(8,128)(2,1)S(1)}, bf16[256,128]{1,0:T(8,128)(2,1)}, u32[]{:S(2)}) copy-start(bf16[256,128]{1,0:T(8,128)(2,1)} %w2_ref.1) | copy-start | bytes 196612
